TPU v7x, 32 devices: a whole 2x2x4 slice. The times are simulated.
32 devices in a mesh: dom: 8 (over z, x), rep: 4 (over y, core).
Axes of the slice: x: 2, y: 2, z: 4, core: 2. Of those that a mesh axis runs over, the one named last changes fastest.
Arguments:
- features: bfloat16 [65536, 128], P('dom'), may hold values from -6 to 6
- weight: bfloat16 [128, 256], replicated, may hold values from -0.5 to 0.5
- out_grad: bfloat16 [65536, 256], P(('dom', 'rep')), may hold values from -6 to 6
- send_rows: int32 [8, 8, 64], P('dom'), may hold values from 0 to 8191, as said below
- send_count: int32 [8, 8], P('dom'), may hold values from 0 to 64, as said below
- tile_target: int32 [8, 4, 256], P('dom', 'rep'), may hold values from 0 to 15, as said below
- tile_source: int32 [8, 4, 256], P('dom', 'rep'), may hold values from 0 to 67, as said below
- tile_weights: bfloat16 [8, 4, 256, 128, 128], P('dom', 'rep'), may hold values from -0.125 to 0.125
Outputs:
- activated: bfloat16 [65536, 256], P(('dom', 'rep'))
- feature_grad: bfloat16 [65536, 128], P(('dom', 'rep'))
- weight_grad: float32 [128, 256], replicated
Inputs may be any that keep to these rules, and one draw needn't show every extreme that they name: Within one list send_rows[o, d] the rows are distinct and increasing; entries at slots c >= send_count[o, d] are ignored. send_count[o, o] is 0. Every owner sends exactly 64 rows to some partition, and every partition receives exactly 64 rows from some owner. `tile_target`: pairs of target and source tiles may repeat. `tile_source`: every halo source tile (64 to 67) is named by some tile of every group.
All inputs are finite; a program needn't handle non-finite values.
Results may differ from a plain program's by a relative error of at most 0.006.
Values may be sent and summed in bfloat16 or wider, within the bound.
No kernel may reach another device: no remote copies, remote signals or barrier semaphores. Data moves between devices by JAX's collectives and lax.ppermute only.
A program may use at most 128 MiB of HBM per device.

v0:
```python
import jax
import jax.numpy as jnp
from jax import lax
from jax.sharding import PartitionSpec as P


def shards(
    features, weight, out_grad, send_rows, send_count, tile_target, tile_source, tile_weights
):
    feat = features.shape[1]
    tile = tile_weights.shape[-1]
    rows = send_rows[0]
    counts = send_count[0]
    width = rows.shape[1]
    valid = jnp.arange(width, dtype=jnp.int32)[None, :] < counts[:, None]
    outgoing = jnp.where(valid[:, :, None], features[rows], jnp.zeros((), jnp.bfloat16))
    halo = lax.all_to_all(outgoing, "dom", split_axis=0, concat_axis=0, tiled=True)
    sources = jnp.concatenate([features, halo.reshape(-1, feat)], axis=0)
    targets = tile_target[0, 0]
    anchors = tile_source[0, 0]
    values = tile_weights[0, 0]
    tgt_count = out_grad.shape[0] // tile
    src_count = sources.shape[0] // tile
    blocks = sources.reshape(src_count, tile, feat)[anchors]
    prods = jnp.einsum("tij,tjf->tif", values, blocks, preferred_element_type=jnp.float32)
    gathered = jax.ops.segment_sum(prods, targets, num_segments=tgt_count)
    gathered = gathered.reshape(-1, feat).astype(jnp.bfloat16)
    pre = jnp.dot(gathered, weight, preferred_element_type=jnp.float32)
    activated = jax.nn.silu(pre).astype(jnp.bfloat16)
    sigma = jax.nn.sigmoid(pre)
    slope = sigma * (1.0 + pre * (1.0 - sigma))
    pre_grad = (out_grad.astype(jnp.float32) * slope).astype(jnp.bfloat16)
    weight_part = jnp.dot(gathered.T, pre_grad, preferred_element_type=jnp.float32)
    weight_grad = lax.psum(weight_part, ("dom", "rep"))
    agg_grad = jnp.dot(pre_grad, weight.T, preferred_element_type=jnp.float32).astype(jnp.bfloat16)
    dblocks = agg_grad.reshape(tgt_count, tile, feat)[targets]
    backward = jnp.einsum("tij,tif->tjf", values, dblocks, preferred_element_type=jnp.float32)
    source_grad = jax.ops.segment_sum(backward, anchors, num_segments=src_count).reshape(-1, feat)
    owned_rows = features.shape[0]
    local = source_grad[:owned_rows]
    incoming = source_grad[owned_rows:].reshape(-1, width, feat)
    returned = lax.all_to_all(incoming, "dom", split_axis=0, concat_axis=0, tiled=True)
    kept = jnp.where(valid[:, :, None], returned, jnp.zeros((), jnp.float32))
    local = local.at[rows.reshape(-1)].add(kept.reshape(-1, feat))
    node_grad = lax.psum_scatter(local, "rep", scatter_dimension=0, tiled=True).astype(jnp.bfloat16)
    return (activated, node_grad, weight_grad)


def solution(mesh):
    return jax.shard_map(
        shards,
        mesh=mesh,
        in_specs=(
            P("dom", None),
            P(),
            P(("dom", "rep"), None),
            P("dom", None, None),
            P("dom", None),
            P("dom", "rep", None),
            P("dom", "rep", None),
            P("dom", "rep", None, None, None),
        ),
        out_specs=(P(("dom", "rep"), None), P(("dom", "rep"), None), P()),
        check_vma=False,
    )
```

profile of v0, /device:TPU:0, one launch (start us, length us, event | category | flops | bytes accessed | tf_op | source)
XLA Modules:
  0.0 379.2 jit_solution(14296807344320537851)
XLA Ops:
  8.0 0.0 copy-start
  8.0 0.8 iota_compare_fusion
  8.8 0.7 compare_select_fusion.1
  9.5 0.1 reshape.170
  9.6 2.9 gather_fusion
  12.5 0.8 broadcast_select_fusion.1
  13.3 7.3 %all-to-all-start = ((bf16[8,64,128]{2,1,0:T(8,128)(2,1)}), bf16[8,64,128]{2,1,0:T(8,128)(2,1)S(1)}, u32[]{:S(2)}, u32[]{:S(2)}) async-start(bf16[8,64,128]{2,1,0:T(8,128)(2,1)} %broadcast_select_fusion.1), calls=%async_computation | async-start | bytes 262144 | tf_op jit(solution)/shard_map/all_to_all | solution.py:17
  20.5 0.7 compare_select_fusion.3
  21.2 0.7 compare_select_fusion.2
  21.9 6.0 %all-to-all-done = bf16[8,64,128]{2,1,0:T(8,128)(2,1)S(1)} async-done(((bf16[8,64,128]{2,1,0:T(8,128)(2,1)}), bf16[8,64,128]{2,1,0:T(8,128)(2,1)S(1)}, u32[]{:S(2)}, u32[]{:S(2)}) %all-to-all-start) | async-done | bytes 131104 | tf_op jit(solution)/shard_map/all_to_all | solution.py:17
  27.9 5.3 %pad_maximum_fusion = bf16[8704,128]{1,0:T(8,128)(2,1)S(1)} fusion(bf16[512,128]{1,0:T(8,128)(2,1)S(1)} %bitcast.45, bf16[8192,128]{1,0:T(8,128)(2,1)} %param.8), kind=kLoop, calls=%fused_computation.11 | loop fusion | flops 4456448 | bytes 4456448 | tf_op jit(solution)/shard_map/concatenate | solution.py:18
  33.2 8.6 %gather_fusion.1 = bf16[256,128,128]{2,1,0:T(8,128)(2,1)} fusion(bf16[68,128,128]{2,1,0:T(8,128)(2,1)S(1)} %bitcast.40, s32[1024]{0:T(1024)S(1)} %pad_clamp_fusion.1), kind=kCustom, calls=%fused_computation.1 | custom fusion | bytes 16778240 | tf_op jit(solution)/shard_map/gather | solution.py:24
  41.9 12.8 %convolution_bitcast_fusion.1 = f32[256,128,128]{1,2,0:T(8,128)} fusion(bf16[256,128,128]{2,1,0:T(8,128)(2,1)} %gather_fusion.1, bf16[1,1,256,128,128]{4,3,2,1,0:T(8,128)(2,1)} %param.15), kind=kOutput, calls=%fused_computation.7 | convolution fusion | flops 1073741824 | bytes 33554432 | tf_op jit(solution)/shard_map/tij,tjf->tif/dot_general | solution.py:25
  54.7 0.0 copy-start.3
  54.7 17.5 %copy.14 = f32[256,128,128]{2,1,0:T(8,128)} copy(f32[256,128,128]{1,2,0:T(8,128)} %convolution_bitcast_fusion.1) | data formatting | bytes 33554432 | tf_op jit(solution)/shard_map/tij,tjf->tif/dot_general | solution.py:25
  72.2 0.1 broadcast_in_dim.35
  72.3 0.0 copy-done.3
  72.3 0.0 copy-start.5
  72.3 33.2 %scatter_fusion = f32[16,128,128]{2,1,0:T(8,128)S(1)} fusion(f32[16,128,128]{2,1,0:T(8,128)S(1)} %broadcast_in_dim.35, s32[256]{0:T(256)S(1)} %bitcast.48, f32[256,128,128]{2,1,0:T(8,128)} %copy.14), kind=kCustom, calls=%fused_computation.3 | custom fusion | flops 4194304 | bytes 50332672 | tf_op jit(solution)/shard_map/scatter-add | solution.py:26
  105.5 0.1 convert_element_type.21
  105.6 0.0 copy-done
  105.6 0.0 copy-done.5
  105.6 2.1 multiply_convert_fusion
  107.7 0.4 convolution_convert_fusion
  108.1 8.8 %gather_fusion.2 = bf16[256,128,128]{2,1,0:T(8,128)(2,1)} fusion(bf16[16,128,128]{2,1,0:T(8,128)(2,1)S(1)} %bitcast.39, s32[1024]{0:T(1024)S(1)} %pad_clamp_fusion), kind=kCustom, calls=%fused_computation.2 | custom fusion | bytes 16778240 | tf_op jit(solution)/shard_map/gather | solution.py:36
  116.9 14.4 %convolution_bitcast_fusion = f32[256,128,128]{1,2,0:T(8,128)} fusion(bf16[256,128,128]{2,1,0:T(8,128)(2,1)} %gather_fusion.2, bf16[1,1,256,128,128]{4,3,2,1,0:T(8,128)(2,1)} %param.15), kind=kOutput, calls=%fused_computation.6 | convolution fusion | flops 1073741824 | bytes 33554432 | tf_op jit(solution)/shard_map/tij,tif->tjf/dot_general | solution.py:37
  131.3 0.0 copy-start.4
  131.3 17.5 %copy.16 = f32[256,128,128]{2,1,0:T(8,128)} copy(f32[256,128,128]{1,2,0:T(8,128)} %convolution_bitcast_fusion) | data formatting | bytes 33554432 | tf_op jit(solution)/shard_map/tij,tif->tjf/dot_general | solution.py:37
  148.8 2.6 broadcast_in_dim.38
  151.3 0.0 copy-done.4
  151.3 0.0 copy-start.2
  151.3 51.9 %scatter_fusion.1 = f32[68,128,128]{2,1,0:T(8,128)} fusion(f32[68,128,128]{2,1,0:T(8,128)} %broadcast_in_dim.38, s32[256]{0:T(256)S(1)} %bitcast.49, f32[256,128,128]{2,1,0:T(8,128)} %copy.16), kind=kCustom, calls=%fused_computation.4 | custom fusion | flops 4194304 | bytes 50332672 | tf_op jit(solution)/shard_map/scatter-add | solution.py:38
  203.3 1.7 slice.20
  204.9 3.4 all-to-all-start.1
  208.4 0.0 reduce-scatter.2.cloned.1.call-start
  208.4 0.0 copy-done.2
  208.4 0.1 reshape_squeeze.3
  208.5 0.0 copy-start.1
  208.5 4.7 %slice.19 = f32[64,128,128]{2,1,0:T(8,128)} slice(f32[68,128,128]{2,1,0:T(8,128)} %scatter_fusion.1), slice={[0:64], [0:128], [0:128]} | slice | bytes 8388608 | tf_op jit(solution)/shard_map/slice | solution.py:40
  213.2 3.4 all-to-all-done.1
  216.5 0.1 broadcast_select_fusion
  216.7 7.1 %scatter_fusion.2 = f32[8192,128]{1,0:T(8,128)} fusion(f32[8192,128]{1,0:T(8,128)} %bitcast.41, s32[512]{0:T(512)S(1)} %bitcast.47, f32[512,128]{1,0:T(8,128)S(1)} %bitcast.44), kind=kCustom, calls=%fused_computation.5 | custom fusion | flops 65536 | bytes 788480 | tf_op jit(solution)/shard_map/scatter-add | solution.py:44
  223.8 0.0 reduce-scatter.2.cloned.1.call-update
  223.8 0.0 all-reduce.2.cloned.1.call-start
  223.8 1.0 fusion.2
  224.9 0.0 all-reduce.2.cloned.1.call-update
  224.9 42.2 %reduce-scatter.2.cloned.1.call-done = f32[2048,128]{1,0:T(8,128)} async-done(((f32[8192,128]{1,0:T(8,128)}), f32[2048,128]{1,0:T(8,128)}) %reduce-scatter.2.cloned.1.call-update) | async-done | bytes 1048592 | tf_op jit(solution)/shard_map/reduce_scatter | solution.py:45
  267.1 2.1 convert_element_type.27
  269.2 101.1 %all-reduce.2.cloned.1.call-done = f32[128,256]{1,0:T(8,128)} async-done(((f32[128,256]{1,0:T(8,128)}), f32[128,256]{1,0:T(8,128)}) %all-reduce.2.cloned.1.call-update) | async-done | bytes 131088 | tf_op jit(solution)/shard_map/psum | solution.py:34
  370.2 1.6 copy.23
  371.8 0.0 copy-done.1
  (4 shorter events, 0.0 us)
Async XLA Ops:
  8.0 97.6 %copy-start = (bf16[128,256]{1,0:T(8,128)(2,1)S(1)}, bf16[128,256]{1,0:T(8,128)(2,1)}, u32[]{:S(2)}) copy-start(bf16[128,256]{1,0:T(8,128)(2,1)} %param.9) | copy-start | bytes 196612
  13.3 14.6 %all-to-all-start = ((bf16[8,64,128]{2,1,0:T(8,128)(2,1)}), bf16[8,64,128]{2,1,0:T(8,128)(2,1)S(1)}, u32[]{:S(2)}, u32[]{:S(2)}) async-start(bf16[8,64,128]{2,1,0:T(8,128)(2,1)} %broadcast_select_fusion.1), calls=%async_computation | async-start | bytes 262144 | tf_op jit(solution)/shard_map/all_to_all | solution.py:17
  54.7 17.6 %copy-start.3 = (s32[1,1,256]{2,1,0:T(1,128)S(1)}, s32[1,1,256]{2,1,0:T(1,128)}, u32[]{:S(2)}) copy-start(s32[1,1,256]{2,1,0:T(1,128)} %param.13) | copy-start | bytes 3076
  72.3 33.3 %copy-start.5 = (bf16[2048,256]{1,0:T(8,128)(2,1)S(1)}, bf16[2048,256]{1,0:T(8,128)(2,1)}, u32[]{:S(2)}) copy-start(bf16[2048,256]{1,0:T(8,128)(2,1)} %param.10) | copy-start | bytes 3145732
  131.3 20.0 %copy-start.4 = (s32[1,1,256]{2,1,0:T(1,128)S(1)}, s32[1,1,256]{2,1,0:T(1,128)}, u32[]{:S(2)}) copy-start(s32[1,1,256]{2,1,0:T(1,128)} %param.14) | copy-start | bytes 3076
  151.3 57.1 %copy-start.2 = (s32[1,8,64]{2,1,0:T(8,128)S(1)}, s32[1,8,64]{2,1,0:T(8,128)}, u32[]{:S(2)}) copy-start(s32[1,8,64]{2,1,0:T(8,128)} %param.11) | copy-start | bytes 6148
  204.9 11.6 %all-to-all-start.1 = ((f32[8,64,128]{2,1,0:T(8,128)}), f32[8,64,128]{2,1,0:T(8,128)S(1)}, u32[]{:S(2)}, u32[]{:S(2)}) async-start(f32[8,64,128]{2,1,0:T(8,128)} %bitcast.18), calls=%async_computation.1 | async-start | bytes 524288 | tf_op jit(solution)/shard_map/all_to_all | solution.py:42
  208.4 58.7 %reduce-scatter.2.cloned.1.call-start = ((), (), s32[]{:S(2)}) async-start(), calls=%async_computation.3 | async-start | bytes 5242880 | tf_op jit(solution)/shard_map/reduce_scatter | solution.py:45
  208.5 163.3 %copy-start.1 = (bf16[128,256]{1,0:T(8,128)(2,1)S(1)}, bf16[128,256]{1,0:T(8,128)(2,1)}, u32[]{:S(2)}) copy-start(bf16[128,256]{1,0:T(8,128)(2,1)} %param.9) | copy-start | bytes 196612
  223.8 146.4 %all-reduce.2.cloned.1.call-start = ((), (), s32[]{:S(2)}) async-start(), calls=%async_computation.4 | async-start | bytes 262144 | tf_op jit(solution)/shard_map/psum | solution.py:34
Sparse Core Ops, SparseCore 0:
  223.9 43.1 reduce-scatter.1
Sparse Core Ops, SparseCore 1:
  230.4 139.8 all-reduce.1
where the time goes:
time: 381 us; the launch traced here: 379 us
  waiting for transfers between devices  153 us (40%)
  other arithmetic  103 us (27%)
  local copies, waits for them, and re-layouts  66 us (17%)
  matrix products  30.7 us (8%)
  between operations  15.6 us (4%)
  starting transfers between devices  10.8 us (3%)
    psum x1, waiting for transfers between devices, shards(): weight_grad = lax.psum(weight_part, ('dom', 'rep'))  101 us
    scatter-add x1, other arithmetic, shards(): jax.ops.segment_sum(backward, anchors, num_segments=src_count)  51.9 us
    reduce_scatter x1, waiting for transfers between devices, shards(): lax.psum_scatter(local, 'rep', scatter_dimension=0, tiled=True)  42.2 us
    scatter-add x1, other arithmetic, shards(): gathered = jax.ops.segment_sum(prods, targets, num_segments=tgt_count)  33.2 us
    dot_general x1, local copies, waits for them, and re-layouts, shards(): jnp.einsum('tij,tjf->tif', values, blocks, preferred_element_type=jnp.flo...  17.5 us
    dot_general x1, local copies, waits for them, and re-layouts, shards(): jnp.einsum('tij,tif->tjf', values, dblocks, preferred_element_type=jnp.fl...  17.5 us
    dot_general x1, matrix products, shards(): jnp.einsum('tij,tif->tjf', values, dblocks, preferred_element_type=jnp.fl...  14.4 us
    dot_general x1, matrix products, shards(): jnp.einsum('tij,tjf->tif', values, blocks, preferred_element_type=jnp.flo...  12.8 us
  transfers between devices with their start and end apart: 4, of which 4 were waited for; matrix products, arithmetic and copies ran while one was open for 2% of the time, Pallas kernels for 0%

commit v1 on v0

v1 whole, which is shorter than its diff:
```python
import functools

import jax
import jax.numpy as jnp
from jax import lax
from jax.experimental import pallas as pl
from jax.experimental.pallas import tpu as pltpu
from jax.sharding import PartitionSpec as P


LANES = 128
BITS_TILE, BITS_OTHER = 10, 7
SIZE = 2
UNROLL_FORWARD, UNROLL_HALO, UNROLL_BACKWARD = 36, 8, 36
PARTS = 8
F32 = jnp.float32
BF16 = jnp.bfloat16
MIB = 1 << 20
VMEM = pl.BlockSpec(memory_space=pltpu.VMEM)
SMEM = pl.BlockSpec(memory_space=pltpu.SMEM)
HBM = pl.BlockSpec(memory_space=pltpu.HBM)
NN = (((1,), (0,)), ((), ()))
NT = (((1,), (1,)), ((), ()))
TN = (((0,), (0,)), ((), ()))


def in_hbm(*arrays):
    return [pltpu.with_memory_space_constraint(x, pltpu.HBM) for x in arrays]


def dot(a, b, dims=NN):
    return lax.dot_general(a, b, dims, preferred_element_type=F32)


def block(i, size):
    return pl.ds(pl.multiple_of(i * size, size), size)


def pick_kernel(rows_in, counts_in, feat_in, out, feat, rows, counts, wide, stage, sems):
    dests, cap = rows.shape
    parts = sems.shape[0] - 2
    step = feat.shape[0] // parts
    small = [
        pltpu.make_async_copy(rows_in, rows, sems.at[parts]),
        pltpu.make_async_copy(counts_in, counts, sems.at[parts + 1]),
    ]
    for copy in small:
        copy.start()

    def fetch(i):
        span = pl.ds(i * step, step)
        return pltpu.make_async_copy(feat_in.at[span], feat.at[span], sems.at[i])

    for i in range(parts):
        fetch(i).start()
    for copy in small:
        copy.wait()
    piece = 256
    for i in range(parts):
        fetch(i).wait()

        def widen(k, carry):
            span = pl.ds(pl.multiple_of(i * step + k * piece, piece), piece)
            wide[span, :] = feat[span, :].astype(F32)
            return carry

        lax.fori_loop(0, step // piece, widen, 0)
    slot = lax.broadcasted_iota(jnp.int32, stage.shape, 0)

    def one(d, carry):
        count = counts[0, d]
        for c in range(cap):
            row = jnp.where(c < count, rows[d, c], 0)
            stage[c : c + 1, :] = wide[pl.ds(row, 1), :]
        out[block(d, cap), :] = jnp.where(slot < count, stage[...], 0.0).astype(BF16)
        return carry

    lax.fori_loop(0, dests, one, 0)


def pick(rows, counts, features):
    dests, cap = rows.shape
    feat = features.shape[1]
    parts = 4
    return pl.pallas_call(
        pick_kernel,
        name="pick",
        out_shape=jax.ShapeDtypeStruct((dests * cap, feat), BF16),
        in_specs=[HBM, HBM, HBM],
        out_specs=VMEM,
        scratch_shapes=[
            pltpu.VMEM(features.shape, BF16),
            pltpu.SMEM(rows.shape, jnp.int32),
            pltpu.SMEM(counts.shape, jnp.int32),
            pltpu.VMEM(features.shape, F32),
            pltpu.VMEM((cap, feat), F32),
            pltpu.SemaphoreType.DMA((parts + 2,)),
        ],
        compiler_params=pltpu.CompilerParams(vmem_limit_bytes=16 * MIB),
        cost_estimate=pl.CostEstimate(
            flops=features.size, bytes_accessed=features.size * 4, transcendentals=0
        ),
    )(*in_hbm(rows, counts, features))


def ordered_sets(key, other, wide):
    count = key.shape[1]
    lanes = jnp.broadcast_to(key, (count, count))
    subs = lanes.T
    i = lax.broadcasted_iota(jnp.int32, (count, count), 0)
    j = lax.broadcasted_iota(jnp.int32, (count, count), 1)
    before = jnp.where((lanes == subs) & (j < i), 1.0, 0.0)
    rank = jnp.sum(before, axis=1, keepdims=True)
    lane = lax.broadcasted_iota(jnp.int32, (count, LANES), 1).astype(F32)
    own = subs[:, :1] == lane
    number = jnp.sum(jnp.where(own, 1.0, 0.0), axis=0, keepdims=True)
    sets = jnp.floor((number + (SIZE - 1.0)) * (1.0 / SIZE))
    k = lax.broadcasted_iota(jnp.int32, (LANES, LANES), 0)
    q = lax.broadcasted_iota(jnp.int32, (LANES, LANES), 1)
    lower = jnp.where(k < q, 1.0, 0.0).astype(BF16)
    starts = dot(jnp.broadcast_to(sets, (16, LANES)).astype(BF16), lower)[:1, :]
    spot = jnp.sum(jnp.where(own, SIZE * starts, 0.0), axis=1, keepdims=True) + rank
    place = lax.broadcasted_iota(jnp.int32, (count, wide), 1).astype(F32)
    chosen = spot == place
    index = lax.broadcasted_iota(jnp.int32, (count, 1), 0).astype(F32) + 1.0
    others = jnp.broadcast_to(other, (count, count)).T[:, :1]
    shift = float(1 << BITS_TILE)
    entry = index + shift * (others + float(1 << BITS_OTHER) * subs[:, :1])
    row = jnp.sum(jnp.where(chosen, entry, 0.0), axis=0, keepdims=True)
    return row.astype(jnp.int32), starts.astype(jnp.int32)


def tile_of(entry):
    return entry & ((1 << BITS_TILE) - 1)


def other_of(entry):
    return (entry >> BITS_TILE) & ((1 << BITS_OTHER) - 1)


def key_of(entry):
    return entry >> (BITS_TILE + BITS_OTHER)


def clear_tiles(acc):
    zeros = jnp.zeros(acc.shape[1:], acc.dtype)

    def clear(k, carry):
        acc[k] = zeros
        return carry

    lax.fori_loop(0, acc.shape[0], clear, 0)


class Plan:
    def __init__(self, ref, base, wide):
        self.ref, self.base, self.wide = ref, base, wide

    def start(self, key):
        return self.ref[0, self.base + self.wide + key]

    def entry(self, at):
        return self.ref[0, self.base + at]


def plans(ref, wide):
    return Plan(ref, 0, wide), Plan(ref, wide + LANES, wide)


def run_sets(plan, first, last, acc, shift, group, product):
    spare = acc.shape[0] - 1
    low, high = plan.start(first), plan.start(last)

    def run(g, carry):
        for u in range(group):
            which = low + g * group + u
            at = SIZE * jnp.minimum(which, high - 1)
            members = [plan.entry(at + i) for i in range(SIZE)]
            place = jnp.where(which < high, key_of(members[0]) - shift, spare)
            acc[place] += product(members)
        return carry

    lax.fori_loop(0, lax.div(high - low + group - 1, group), run, 0)


def gather_product(held, rows):
    tile = held.shape[-1]

    def product(members):
        left = jnp.concatenate([held[tile_of(e)] for e in members], axis=1)
        right = jnp.concatenate([rows[block(other_of(e), tile), :] for e in members], axis=0)
        return dot(left, right)

    return product


def scatter_product(held, grads):
    def product(members):
        left = jnp.concatenate([grads[other_of(e)] for e in members], axis=1)
        right = jnp.concatenate([held[tile_of(e)] for e in members], axis=0)
        return dot(left, right)

    return product


def tile_copies(tiles, held, sems):
    step = tiles.shape[0] // PARTS
    return [
        pltpu.make_async_copy(
            tiles.at[pl.ds(i * step, step)], held.at[pl.ds(1 + i * step, step)], sems.at[i]
        )
        for i in range(PARTS)
    ]


def start_all(copies):
    for copy in copies:
        copy.start()


def wait_all(copies):
    for copy in copies:
        copy.wait()


def forward_kernel(
    ranks, halos, source_in, target_in, feat_in, tiles, acc, made, held, feat, source, target, table, sems
):
    count, tile, _ = tiles.shape
    local = feat.shape[0] // tile
    targets = acc.shape[0] - 1
    quarter = local // ranks
    small = [
        pltpu.make_async_copy(source_in, source, sems.at[PARTS]),
        pltpu.make_async_copy(target_in, target, sems.at[PARTS + 1]),
    ]
    start_all(small)
    large = [pltpu.make_async_copy(feat_in, feat, sems.at[PARTS + 2])]
    large += tile_copies(tiles, held, sems)
    start_all(large)
    wait_all(small)
    held[0] = jnp.zeros((tile, tile), BF16)
    wide = made.shape[1] // 2 - LANES
    ahead, _ = plans(table, wide)
    src, tgt = source[...], target[...]
    mine = src < local
    late = lax.broadcasted_iota(jnp.int32, src.shape, 1) >= count // 2
    key = jnp.where(mine, jnp.where(late, targets + tgt, tgt), 2 * targets + tgt).astype(F32)
    other = jnp.where(mine, src, src - local).astype(F32)
    made_ahead = ordered_sets(key, other, wide)
    me = lax.axis_index("rep")
    part = jnp.zeros_like(src)
    for k in range(1, ranks):
        part = part + jnp.where(src >= k * quarter, 1, 0)
    place = (part ^ (me ^ (ranks - 1))) * quarter + (src - part * quarter)
    key = jnp.where(mine, halos + place, src - local).astype(F32)
    made_back = ordered_sets(key, tgt.astype(F32), wide)
    made[...] = jnp.concatenate(made_ahead + made_back, axis=1)
    order = pltpu.make_async_copy(made, table, sems.at[PARTS])
    order.start()
    clear_tiles(acc)
    order.wait()
    half = 1 + PARTS // 2
    product = gather_product(held, feat)
    wait_all(large[:half])
    run_sets(ahead, 0, targets, acc, 0, UNROLL_FORWARD, product)
    wait_all(large[half:])
    run_sets(ahead, targets, 2 * targets, acc, targets, UNROLL_FORWARD, product)


def forward(source, target, features, tiles, targets, ranks, halos):
    count, tile, _ = tiles.shape
    feat = features.shape[1]
    wide = count + LANES
    return pl.pallas_call(
        functools.partial(forward_kernel, ranks, halos),
        name="forward",
        out_shape=(
            pltpu.HBM((targets + 1, tile, feat), F32),
            pltpu.VMEM((1, 2 * (wide + LANES)), jnp.int32),
        ),
        in_specs=[HBM, HBM, HBM, HBM],
        out_specs=(VMEM, VMEM),
        scratch_shapes=[
            pltpu.VMEM((count + 1, tile, tile), BF16),
            pltpu.VMEM(features.shape, BF16),
            pltpu.VMEM((1, count), jnp.int32),
            pltpu.VMEM((1, count), jnp.int32),
            pltpu.SMEM((1, 2 * (wide + LANES)), jnp.int32),
            pltpu.SemaphoreType.DMA((PARTS + 3,)),
        ],
        compiler_params=pltpu.CompilerParams(vmem_limit_bytes=20 * MIB),
        cost_estimate=pl.CostEstimate(
            flops=2 * tiles.size * feat * 4, bytes_accessed=tiles.size * 2, transcendentals=0
        ),
    )(*in_hbm(source, target, features, tiles))


def middle_kernel(
    table, acc_in, halo, weight, out_grad_in, tiles, act, wgrad, back, sent_a, kept_a, sent_b, kept_b,
    held, some, rows, sums, hsum, lsum, grads, acc, out_grad, sems, few
):
    _, tile, _ = tiles.shape
    targets = acc.shape[0]
    halos = halo.shape[0] // tile
    ahead, order = plans(table, table.shape[1] // 2 - LANES)
    low, high = ahead.start(2 * targets), ahead.start(3 * targets)
    groups = lax.div(high - low + UNROLL_HALO - 1, UNROLL_HALO)
    batch = SIZE * UNROLL_HALO

    def entry_of(n, i):
        return ahead.entry(jnp.minimum(SIZE * low + n * batch + i, SIZE * high - 1))

    def fetch(n, carry):
        for i in range(batch):
            t = jnp.maximum(tile_of(entry_of(n, i)), 1) - 1
            pltpu.make_async_copy(tiles.at[t], some.at[n * batch + i], few.at[n]).start()
        return carry

    lax.fori_loop(0, groups, fetch, 0)
    inputs = [
        pltpu.make_async_copy(acc_in.at[pl.ds(0, targets)], acc, sems.at[PARTS]),
        pltpu.make_async_copy(out_grad_in, out_grad, sems.at[PARTS + 1]),
    ]
    large = tile_copies(tiles, held, sems)
    start_all(inputs + large)
    held[0] = jnp.zeros((tile, tile), BF16)
    clear_tiles(sums)
    clear_tiles(hsum)
    clear_tiles(lsum)
    rows[: halos * tile, :] = halo[...]
    rows[halos * tile :, :] = jnp.zeros((tile, halo.shape[1]), BF16)

    def add(n, carry):
        span = block(n, batch)
        pltpu.make_async_copy(tiles.at[pl.ds(0, batch)], some.at[span], few.at[n]).wait()
        for u in range(UNROLL_HALO):
            left, right = [], []
            for i in range(SIZE * u, SIZE * u + SIZE):
                entry = entry_of(n, i)
                s = jnp.where(tile_of(entry) > 0, other_of(entry), halos)
                left.append(some[n * batch + i])
                right.append(rows[block(s, tile), :])
            here = low + n * UNROLL_HALO + u < high
            place = jnp.where(here, key_of(entry_of(n, SIZE * u)) - 2 * targets, targets)
            sums[place] += dot(jnp.concatenate(left, axis=1), jnp.concatenate(right, axis=0))
        return carry

    lax.fori_loop(0, groups, add, 0)
    wgrad[...] = jnp.zeros(wgrad.shape, F32)
    wait_all(inputs)
    width = 4

    def dense(b, carry):
        many = []
        for u in range(width):
            k = b * width + u
            many.append((acc[k] + sums[k]).astype(BF16))
        packed = jnp.concatenate(many, axis=0)
        span = block(b, width * tile)
        pre = dot(packed, weight[...])
        sigma = jax.nn.sigmoid(pre)
        silu = pre * sigma
        act[span, :] = silu.astype(BF16)
        slope = sigma + silu * (1.0 - sigma)
        pre_grad = (out_grad[span, :].astype(F32) * slope).astype(BF16)
        wgrad[...] += dot(packed, pre_grad, TN)
        turned = dot(weight[...], pre_grad, NT).astype(BF16)
        for u in range(width):
            grads[b * width + u] = turned[:, u * tile : (u + 1) * tile]
        return carry

    lax.fori_loop(0, targets // width, dense, 0)
    wait_all(large)
    product = scatter_product(held, grads)
    run_sets(order, 0, halos, hsum, 0, UNROLL_HALO, product)

    def turn(s, carry):
        back[block(s, tile), :] = hsum[s].T.astype(BF16)
        return carry

    lax.fori_loop(0, halos, turn, 0)
    part = sent_a.shape[0]
    run_sets(order, halos, halos + 4 * part, lsum, halos, UNROLL_BACKWARD, product)

    def flush(k, carry):
        sent_a[k] = lsum[k].astype(BF16)
        kept_a[k] = lsum[part + k]
        sent_b[k] = lsum[2 * part + k].astype(BF16)
        kept_b[k] = lsum[3 * part + k]
        return carry

    lax.fori_loop(0, part, flush, 0)


def middle(table, acc, halo, weight, out_grad, tiles, quarter):
    count, tile, _ = tiles.shape
    targets = acc.shape[0] - 1
    feat, hidden = weight.shape
    batch = SIZE * UNROLL_HALO
    groups = (count + targets + batch - 1) // batch
    return pl.pallas_call(
        middle_kernel,
        name="middle",
        out_shape=(
            jax.ShapeDtypeStruct(out_grad.shape, BF16),
            jax.ShapeDtypeStruct((feat, hidden), F32),
            jax.ShapeDtypeStruct(halo.shape, BF16),
            jax.ShapeDtypeStruct((quarter, feat, tile), BF16),
            pltpu.VMEM((quarter, feat, tile), F32),
            jax.ShapeDtypeStruct((quarter, feat, tile), BF16),
            pltpu.HBM((quarter, feat, tile), F32),
        ),
        in_specs=[SMEM, HBM, VMEM, VMEM, HBM, HBM],
        out_specs=(VMEM,) * 7,
        scratch_shapes=[
            pltpu.VMEM((count + 1, tile, tile), BF16),
            pltpu.VMEM((groups * batch, tile, tile), BF16),
            pltpu.VMEM((halo.shape[0] + tile, feat), BF16),
            pltpu.VMEM((targets + 1, tile, feat), F32),
            pltpu.VMEM((halo.shape[0] // tile + 1, feat, tile), F32),
            pltpu.VMEM((4 * quarter + 1, feat, tile), F32),
            pltpu.VMEM((targets, feat, tile), BF16),
            pltpu.VMEM((targets, tile, feat), F32),
            pltpu.VMEM(out_grad.shape, BF16),
            pltpu.SemaphoreType.DMA((PARTS + 2,)),
            pltpu.SemaphoreType.DMA((groups,)),
        ],
        compiler_params=pltpu.CompilerParams(vmem_limit_bytes=40 * MIB),
        cost_estimate=pl.CostEstimate(
            flops=6 * out_grad.size * feat * 2 + tiles.size * feat * 8,
            bytes_accessed=out_grad.size * 8,
            transcendentals=out_grad.size,
        ),
    )(table, *in_hbm(acc), halo, weight, *in_hbm(out_grad, tiles))


def finish_kernel(index, kept, near, far, here, there, out, both):
    count, feat, tile = kept.shape
    base = lax.axis_index("rep") * (count * tile)
    slots = index.shape[1]
    sub = lax.broadcasted_iota(jnp.int32, (tile, slots), 0)
    both[:, :feat] = here[...]
    both[:, feat:] = there[...]
    width = 4

    def one(b, carry):
        for u in range(width):
            k = b * width + u
            total = kept[k] + near[k].astype(F32) + far[k].astype(F32)
            hit = jnp.where(index[...] - (base + k * tile) == sub, 1.0, 0.0).astype(BF16)
            extra = dot(hit, both[...])
            out[block(k, tile), :] = (total.T + extra[:, :feat] + extra[:, feat:]).astype(BF16)
        return carry

    lax.fori_loop(0, count // width, one, 0)


def finish(index, kept, near, far, here, there):
    count, feat, tile = kept.shape
    return pl.pallas_call(
        finish_kernel,
        name="finish",
        out_shape=jax.ShapeDtypeStruct((count * tile, feat), BF16),
        in_specs=[VMEM] * 6,
        out_specs=VMEM,
        scratch_shapes=[pltpu.VMEM((here.shape[0], 2 * feat), BF16)],
        compiler_params=pltpu.CompilerParams(vmem_limit_bytes=24 * MIB),
        cost_estimate=pl.CostEstimate(
            flops=4 * count * tile * feat * index.shape[1],
            bytes_accessed=kept.size * 10,
            transcendentals=0,
        ),
    )(index, kept, near, far, here, there)


def swap(x, axis, size, bit):
    return lax.ppermute(x, axis, [(i, i ^ bit) for i in range(size)])


def plus(x, y):
    return x + y


def exchange(x):
    return lax.all_to_all(x, "dom", split_axis=0, concat_axis=0, tiled=True)


def pick_one(blocks, i):
    return lax.dynamic_index_in_dim(blocks, i, 0, False)


def join(bit, mine, other):
    first = jnp.where(bit == 0, mine, other)
    second = jnp.where(bit == 0, other, mine)
    return jnp.concatenate([first, second], axis=0)


def shards(n_dom, n_rep, features, weight, out_grad, send_rows, send_count, tile_target, tile_source, tile_weights):
    assert n_rep == 4 and n_dom & (n_dom - 1) == 0
    feat = features.shape[1]
    tiles = tile_weights[0, 0]
    tile = tiles.shape[-1]
    rows = send_rows[0]
    cap = rows.shape[1]
    targets = out_grad.shape[0] // tile
    local = features.shape[0] // tile
    halo_tiles = n_dom * cap // tile
    quarter = local // n_rep
    count, most = tiles.shape[0], halo_tiles + local
    assert count % 8 == 0 and count < 1 << BITS_TILE and max(most, 3 * targets) < LANES
    source, target = tile_source[0], tile_target[0]

    outgoing = pick(rows, send_count, features).reshape(n_dom, cap, feat)
    halo = exchange(outgoing).reshape(-1, feat)
    acc, table = forward(source, target, features, tiles, targets, n_rep, halo_tiles)
    activated, wpart, back, sent_a, kept_a, sent_b, kept_b = middle(
        table, acc, halo, weight, out_grad, tiles, quarter
    )

    me = lax.axis_index("rep")
    low_bit = me & 1
    hidden = weight.shape[1]

    near_a = swap(sent_a, "rep", n_rep, 1)
    near_b = swap(sent_b, "rep", n_rep, 1)
    across = (kept_a + near_a.astype(F32)).astype(BF16)
    far = swap(across, "rep", n_rep, 2)

    returned = exchange(back.reshape(n_dom, cap, feat)).reshape(-1, feat)
    beside = swap(returned, "rep", n_rep, 1)
    here = (returned.astype(F32) + beside.astype(F32)).astype(BF16)
    there = swap(here, "rep", n_rep, 2)

    halves = wpart.reshape(2, feat // 2, hidden)
    near = swap(pick_one(halves, 1 - low_bit), "rep", n_rep, 1)
    total = plus(pick_one(halves, low_bit), near)
    total = plus(total, swap(total, "rep", n_rep, 2))
    bit = 1
    while bit < n_dom:
        total = plus(total, swap(total, "dom", n_dom, bit))
        bit *= 2
    weight_grad = join(low_bit, total, swap(total, "rep", n_rep, 1))

    valid = jnp.arange(cap, dtype=jnp.int32)[None, :] < send_count[0][:, None]
    index = jnp.where(valid, rows, -1).reshape(1, -1)
    node_grad = finish(index, kept_b, near_b, far, here, there)
    return (activated, node_grad, weight_grad)


def solution(mesh):
    def body(*args):
        return shards(mesh.shape["dom"], mesh.shape["rep"], *args)

    return jax.shard_map(
        body,
        mesh=mesh,
        in_specs=(
            P("dom", None),
            P(),
            P(("dom", "rep"), None),
            P("dom", None, None),
            P("dom", None),
            P("dom", "rep", None),
            P("dom", "rep", None),
            P("dom", "rep", None, None, None),
        ),
        out_specs=(P(("dom", "rep"), None), P(("dom", "rep"), None), P()),
        check_vma=False,
    )
```

time: 381 us -> 77.2 us (0.20)
  waiting for transfers between devices: 153 us -> 23.2 us
  other arithmetic: 103 us -> 2.02 us
  local copies, waits for them, and re-layouts: 66 us -> 0.2 us
  matrix products: 30.7 us -> 0 us
  Pallas kernels: 0 us -> 24.3 us
  starting transfers between devices: 10.8 us -> 26.3 us
  between operations: 15.6 us -> 0.8 us
    psum x1 -> x0, waiting for transfers between devices: 101 us -> none  [shards(): weight_grad = lax.psum(weight_part, ('dom', 'rep'))]
    scatter-add x3 -> x0, other arithmetic: 92.2 us -> none  [the longest x1 51.9 us: shards(): jax.ops.segment_sum(backward, anchors, num_segments=src_count)]
    reduce_scatter x1 -> x0, waiting for transfers between devices: 42.2 us -> none  [shards(): lax.psum_scatter(local, 'rep', scatter_dimension=0, tiled=True)]
    dot_general x2 -> x0, local copies, waits for them, and re-layouts: 34.9 us -> none  [the longest x1 17.5 us: shards(): jnp.einsum('tij,tjf->tif', values, blocks, preferred_element_type=jnp.flo...]
    dot_general x5 -> x0, matrix products: 30.7 us -> none  [the longest x1 14.4 us: shards(): jnp.einsum('tij,tif->tjf', values, dblocks, preferred_element_type=jnp.fl...]
    pallas_call x0 -> x4, Pallas kernels: none -> 24.3 us  [the longest x1 11.6 us: middle(): pl.pallas_call(middle_kernel, name='middle', out_shape=(jax.ShapeDtypeStr...]
    ppermute x0 -> x11, waiting for transfers between devices: none -> 23.2 us  [swap(): return lax.ppermute(x, axis, [(i, i ^ bit) for i in range(size)])]
    gather x3 -> x0, local copies, waits for them, and re-layouts: 20.3 us -> none  [the longest x1 8.79 us: shards(): dblocks = agg_grad.reshape(tgt_count, tile, feat)[targets]]
  transfers between devices with their start and end apart: 4 -> 13, of which waited for: 4 -> 5; matrix products, arithmetic and copies ran while one was open for 2% -> 3% of each run, Pallas kernels for 0% -> 10%
where the time goes in v1:
time: 77.2 us; the launch traced here: 76.8 us
  starting transfers between devices  26.3 us (34%)
  Pallas kernels  24.3 us (31%)
  waiting for transfers between devices  23.2 us (30%)
  other arithmetic  2.02 us (3%)
  between operations  0.8 us (1%)
    ppermute x11, waiting for transfers between devices, swap(): return lax.ppermute(x, axis, [(i, i ^ bit) for i in range(size)])  23.2 us
    all_to_all x2, starting transfers between devices, exchange(): return lax.all_to_all(x, 'dom', split_axis=0, concat_axis=0, tiled=True)  13.5 us
    ppermute x11, starting transfers between devices, swap(): return lax.ppermute(x, axis, [(i, i ^ bit) for i in range(size)])  12.8 us
    pallas_call x1, Pallas kernels, middle(): pl.pallas_call(middle_kernel, name='middle', out_shape=(jax.ShapeDtypeStr...  11.6 us
    pallas_call x1, Pallas kernels, forward(): pl.pallas_call(functools.partial(forward_kernel, ranks, halos), name='for...  7.49 us
    pallas_call x1, Pallas kernels, pick(): pl.pallas_call(pick_kernel, name='pick', out_shape=jax.ShapeDtypeStruct((...  3.06 us
    pallas_call x1, Pallas kernels, finish(): pl.pallas_call(finish_kernel, name='finish', out_shape=jax.ShapeDtypeStru...  2.15 us
  transfers between devices with their start and end apart: 13, of which 5 were waited for; matrix products, arithmetic and copies ran while one was open for 3% of the time, Pallas kernels for 10%

profile of v1, /device:TPU:0, one launch (start us, length us, event | category | flops | bytes accessed | tf_op | source)
XLA Modules:
  0.0 76.8 jit_solution(12577796952262371913)
XLA Ops:
  0.6 3.1 %pick.1 = bf16[512,128]{1,0:T(8,128)(2,1)} custom-call(s32[8,64]{1,0:T(8,128)} %bitcast.19, s32[1,8]{1,0:T(1,128)} %counts_in.1, bf16[8192,128]{1,0:T(8,128)(2,1)} %feat_in.3), custom_call_target="tpu_custom_call" | custom-call | flops 1048576 | bytes 4194304 | tf_op jit(solution)/shard_map/pick/pallas_call | solution.py:85
  3.7 7.3 %all-to-all-start = ((bf16[8,64,128]{2,1,0:T(8,128)(2,1)}), bf16[8,64,128]{2,1,0:T(8,128)(2,1)S(1)}, u32[]{:S(2)}, u32[]{:S(2)}) async-start(bf16[8,64,128]{2,1,0:T(8,128)(2,1)} %bitcast.4), calls=%async_computation | async-start | bytes 262144 | tf_op jit(solution)/shard_map/all_to_all | solution.py:486
  11.0 0.0 copy-start.1
  11.0 7.5 %forward.1 = (f32[17,128,128]{2,1,0:T(8,128)}, s32[1,1024]{1,0:T(1,128)S(1)}) custom-call(s32[1,256]{1,0:T(1,128)} %bitcast.23, s32[1,256]{1,0:T(1,128)} %bitcast.24, bf16[8192,128]{1,0:T(8,128)(2,1)} %feat_in.3, bf16[256,128,128]{2,1,0:T(8,128)(2,1)} %bitcast.21), custom_call_target="tpu_custom_call" | custom-call | flops 4294967296 | bytes 8388608 | tf_op jit(solution)/shard_map/forward/pallas_call | solution.py:275
  18.5 0.0 all-to-all-done
  18.5 0.0 copy-done.1
  18.5 0.0 copy-start.3
  18.5 0.0 copy-start.2
  18.5 11.6 %middle.1 = (bf16[2048,256]{1,0:T(8,128)(2,1)}, f32[128,256]{1,0:T(8,128)S(1)}, bf16[512,128]{1,0:T(8,128)(2,1)}, bf16[16,128,128]{2,1,0:T(8,128)(2,1)}, f32[16,...) custom-call(s32[1,1024]{1,0:T(1,128)S(1)} %get-tuple-element.12.table, ...), custom_call_target="tpu_custom_call" | custom-call | flops 5100273664 | bytes 4194304 | tf_op jit(solution)/shard_map/middle/pallas_call | solution.py:402
  30.1 0.1 collective-permute-start.5
  30.2 1.2 %collective-permute-done.5 = f32[64,256]{1,0:T(8,128)S(1)} collective-permute-done((f32[64,256]{1,0:T(8,128)S(1)}, f32[64,256]{1,0:T(8,128)S(1)}, u32[]{:S(2)}, u32[]{:S(2)}) %collective-permute-start.5) | collective-permute-done | bytes 65568 | tf_op jit(solution)/shard_map/ppermute | solution.py:478
  31.5 0.0 copy-start
  31.5 1.6 %collective-permute-start.6 = (f32[64,256]{1,0:T(8,128)S(1)}, f32[64,256]{1,0:T(8,128)S(1)}, u32[]{:S(2)}, u32[]{:S(2)}) collective-permute-start(f32[64,256]{1,0:T(8,128)S(1)} %bitcast_add_fusion), channel_id=1, source_target_pairs={{0,2},{1,3},{2,0},{3,1},{4,6},{5,7},{6,4},{7,5},{8,10},{9,11},{10,... | collective-permute-start | bytes 196616 | tf_op jit(solution)/shard_map/ppermute | solution.py:478
  33.0 0.0 collective-permute-start.1
  33.1 2.7 %collective-permute-done.6 = f32[64,256]{1,0:T(8,128)S(1)} collective-permute-done((f32[64,256]{1,0:T(8,128)S(1)}, f32[64,256]{1,0:T(8,128)S(1)}, u32[]{:S(2)}, u32[]{:S(2)}) %collective-permute-start.6) | collective-permute-done | bytes 65568 | tf_op jit(solution)/shard_map/ppermute | solution.py:478
  35.8 2.5 %collective-permute-start.7 = (f32[64,256]{1,0:T(8,128)S(1)}, f32[64,256]{1,0:T(8,128)S(1)}, u32[]{:S(2)}, u32[]{:S(2)}) collective-permute-start(f32[64,256]{1,0:T(8,128)S(1)} %add.34), channel_id=1, source_target_pairs={{0,4},{4,0},{8,12},{12,8},{16,20},{20,16},{24,28},{28,24},{1,5},{5... | collective-permute-start | bytes 196616 | tf_op jit(solution)/shard_map/ppermute | solution.py:478
  38.3 6.2 %all-to-all-start.1 = ((bf16[8,64,128]{2,1,0:T(8,128)(2,1)}), bf16[8,64,128]{2,1,0:T(8,128)(2,1)S(1)}, u32[]{:S(2)}, u32[]{:S(2)}) async-start(bf16[8,64,128]{2,1,0:T(8,128)(2,1)} %bitcast.7), calls=%async_computation.1 | async-start | bytes 262144 | tf_op jit(solution)/shard_map/all_to_all | solution.py:486
  44.5 0.0 collective-permute-done.7
  44.6 2.1 %collective-permute-start.8 = (f32[64,256]{1,0:T(8,128)S(1)}, f32[64,256]{1,0:T(8,128)S(1)}, u32[]{:S(2)}, u32[]{:S(2)}) collective-permute-start(f32[64,256]{1,0:T(8,128)S(1)} %add.35), channel_id=1, source_target_pairs={{0,8},{4,12},{8,0},{12,4},{16,24},{20,28},{24,16},{28,20},{1,9},{5... | collective-permute-start | bytes 196616 | tf_op jit(solution)/shard_map/ppermute | solution.py:478
  46.6 0.0 copy-done.3
  46.6 0.1 iota_compare_fusion
  46.7 0.0 copy-done.2
  46.7 0.1 squeeze.25
  46.8 0.1 lt.36
  46.9 2.5 %collective-permute-done.8 = f32[64,256]{1,0:T(8,128)S(1)} collective-permute-done((f32[64,256]{1,0:T(8,128)S(1)}, f32[64,256]{1,0:T(8,128)S(1)}, u32[]{:S(2)}, u32[]{:S(2)}) %collective-permute-start.8) | collective-permute-done | bytes 65568 | tf_op jit(solution)/shard_map/ppermute | solution.py:478
  49.4 3.8 %collective-permute-start.9 = (f32[64,256]{1,0:T(8,128)S(1)}, f32[64,256]{1,0:T(8,128)S(1)}, u32[]{:S(2)}, u32[]{:S(2)}) collective-permute-start(f32[64,256]{1,0:T(8,128)S(1)} %add.36), channel_id=1, source_target_pairs={{0,16},{4,20},{8,24},{12,28},{16,0},{20,4},{24,8},{28,12},{1,17},{... | collective-permute-start | bytes 196616 | tf_op jit(solution)/shard_map/ppermute | solution.py:478
  53.2 0.0 collective-permute-start
  53.2 0.0 all-to-all-done.1
  53.2 0.5 collective-permute-start.3
  53.7 2.4 %collective-permute-done.9 = f32[64,256]{1,0:T(8,128)S(1)} collective-permute-done((f32[64,256]{1,0:T(8,128)S(1)}, f32[64,256]{1,0:T(8,128)S(1)}, u32[]{:S(2)}, u32[]{:S(2)}) %collective-permute-start.9) | collective-permute-done | bytes 65568 | tf_op jit(solution)/shard_map/ppermute | solution.py:478
  56.2 0.1 collective-permute-start.10
  56.2 0.0 collective-permute-done.1
  56.2 1.2 %add_convert_fusion = bf16[16,128,128]{2,1,0:T(8,128)(2,1)S(1)} fusion(f32[16,128,128]{2,1,0:T(8,128)S(1)} %get-tuple-element.17, bf16[16,128,128]{2,1,0:T(8,128)(2,1)} %collective-permute-done.1), kind=kLoop, calls=%fused_computation | loop fusion | flops 786432 | bytes 2097152 | tf_op jit(solution)/shard_map/convert_element_type | solution.py:527
  57.4 0.1 collective-permute-start.2
  57.5 0.0 collective-permute-done.3
  57.6 2.1 %collective-permute-start.4 = (bf16[512,128]{1,0:T(8,128)(2,1)S(1)}, bf16[512,128]{1,0:T(8,128)(2,1)S(1)}, u32[]{:S(2)}, u32[]{:S(2)}) collective-permute-start(bf16[512,128]{1,0:T(8,128)(2,1)S(1)} %add_convert_fusion.1.here), channel_id=1, source_target_pairs={{0,2},{1,3},{2,0},{3,1},{4,6},{5,7},{6,4},{7,5},{8,10},{9,11},{10,... | collective-permute-start | bytes 393224 | tf_op jit(solution)/shard_map/ppermute | solution.py:478
  59.6 0.0 collective-permute-done.10
  59.6 0.7 pad_maximum_fusion
  60.3 14.3 %collective-permute-done.4.there = bf16[512,128]{1,0:T(8,128)(2,1)S(1)} collective-permute-done((bf16[512,128]{1,0:T(8,128)(2,1)S(1)}, bf16[512,128]{1,0:T(8,128)(2,1)S(1)}, u32[]{:S(2)}, u32[]{:S(2)}) %collective-permute-start.4) | collective-permute-done | bytes 131104 | tf_op jit(solution)/shard_map/ppermute | solution.py:478
  74.6 0.0 collective-permute-done.near
  74.6 0.0 collective-permute-done.2.far
  74.6 0.0 copy-done
  74.6 2.2 %finish.1 = bf16[2048,128]{1,0:T(8,128)(2,1)} custom-call(s32[1,512]{1,0:T(1,128)S(1)} %broadcast_select_fusion.2.index, f32[16,128,128]{2,1,0:T(8,128)S(1)} %copy-done, bf16[16,128,128]{2,1,0:T(8,128)(2,1)S(1)} %collective-permute-done.near, bf16[16,128,128]{2,1,0:T(8,128)(2,1)S(1)} %collective-permute-done.2.far, ...), custom_call_target="tpu_custom_call" | custom-call | flops 536870912 | bytes 2621440 | tf_op jit(solution)/shard_map/finish/pallas_call | solution.py:461
  (9 shorter events, 0.1 us)
Async XLA Ops:
  3.7 14.8 %all-to-all-start = ((bf16[8,64,128]{2,1,0:T(8,128)(2,1)}), bf16[8,64,128]{2,1,0:T(8,128)(2,1)S(1)}, u32[]{:S(2)}, u32[]{:S(2)}) async-start(bf16[8,64,128]{2,1,0:T(8,128)(2,1)} %bitcast.4), calls=%async_computation | async-start | bytes 262144 | tf_op jit(solution)/shard_map/all_to_all | solution.py:486
  11.0 7.5 %copy-start.1 = (bf16[128,256]{1,0:T(8,128)(2,1)S(1)}, bf16[128,256]{1,0:T(8,128)(2,1)}, u32[]{:S(2)}) copy-start(bf16[128,256]{1,0:T(8,128)(2,1)} %weight.1) | copy-start | bytes 196612
  18.5 28.1 %copy-start.3 = (s32[1,8]{1,0:T(1,128)S(1)}, s32[1,8]{1,0:T(1,128)}, u32[]{:S(2)}) copy-start(s32[1,8]{1,0:T(1,128)} %counts_in.1) | copy-start | bytes 100
  18.5 28.2 %copy-start.2 = (s32[1,8,64]{2,1,0:T(8,128)S(1)}, s32[1,8,64]{2,1,0:T(8,128)}, u32[]{:S(2)}) copy-start(s32[1,8,64]{2,1,0:T(8,128)} %param.11) | copy-start | bytes 6148
  30.1 1.3 %collective-permute-start.5 = (f32[64,256]{1,0:T(8,128)S(1)}, f32[64,256]{1,0:T(8,128)S(1)}, u32[]{:S(2)}, u32[]{:S(2)}) collective-permute-start(f32[64,256]{1,0:T(8,128)S(1)} %dynamic-slice_bitcast_fusion), channel_id=1, source_target_pairs={{0,1},{1,0},{2,3},{3,2},{4,5},{5,4},{6,7},{7,6},{8,9},{9,8},{10,11... | collective-permute-start | bytes 196616 | tf_op jit(solution)/shard_map/ppermute | solution.py:478
  31.5 43.1 %copy-start = (f32[16,128,128]{2,1,0:T(8,128)S(1)}, f32[16,128,128]{2,1,0:T(8,128)}, u32[]{:S(2)}) copy-start(f32[16,128,128]{2,1,0:T(8,128)} %get-tuple-element.15.kept) | copy-start | bytes 3145732
  31.5 4.3 %collective-permute-start.6 = (f32[64,256]{1,0:T(8,128)S(1)}, f32[64,256]{1,0:T(8,128)S(1)}, u32[]{:S(2)}, u32[]{:S(2)}) collective-permute-start(f32[64,256]{1,0:T(8,128)S(1)} %bitcast_add_fusion), channel_id=1, source_target_pairs={{0,2},{1,3},{2,0},{3,1},{4,6},{5,7},{6,4},{7,5},{8,10},{9,11},{10,... | collective-permute-start | bytes 196616 | tf_op jit(solution)/shard_map/ppermute | solution.py:478
  33.0 23.2 %collective-permute-start.1 = (bf16[16,128,128]{2,1,0:T(8,128)(2,1)}, bf16[16,128,128]{2,1,0:T(8,128)(2,1)}, u32[]{:S(2)}, u32[]{:S(2)}) collective-permute-start(bf16[16,128,128]{2,1,0:T(8,128)(2,1)} %get-tuple-element.18), channel_id=1, source_target_pairs={{0,1},{1,0},{2,3},{3,2},{4,5},{5,4},{6,7},{7,6},{8,9},{9,8},{10,11... | collective-permute-start | bytes 1572872 | tf_op jit(solution)/shard_map/ppermute | solution.py:478
  35.8 8.7 %collective-permute-start.7 = (f32[64,256]{1,0:T(8,128)S(1)}, f32[64,256]{1,0:T(8,128)S(1)}, u32[]{:S(2)}, u32[]{:S(2)}) collective-permute-start(f32[64,256]{1,0:T(8,128)S(1)} %add.34), channel_id=1, source_target_pairs={{0,4},{4,0},{8,12},{12,8},{16,20},{20,16},{24,28},{28,24},{1,5},{5... | collective-permute-start | bytes 196616 | tf_op jit(solution)/shard_map/ppermute | solution.py:478
  38.3 14.9 %all-to-all-start.1 = ((bf16[8,64,128]{2,1,0:T(8,128)(2,1)}), bf16[8,64,128]{2,1,0:T(8,128)(2,1)S(1)}, u32[]{:S(2)}, u32[]{:S(2)}) async-start(bf16[8,64,128]{2,1,0:T(8,128)(2,1)} %bitcast.7), calls=%async_computation.1 | async-start | bytes 262144 | tf_op jit(solution)/shard_map/all_to_all | solution.py:486
  44.6 4.8 %collective-permute-start.8 = (f32[64,256]{1,0:T(8,128)S(1)}, f32[64,256]{1,0:T(8,128)S(1)}, u32[]{:S(2)}, u32[]{:S(2)}) collective-permute-start(f32[64,256]{1,0:T(8,128)S(1)} %add.35), channel_id=1, source_target_pairs={{0,8},{4,12},{8,0},{12,4},{16,24},{20,28},{24,16},{28,20},{1,9},{5... | collective-permute-start | bytes 196616 | tf_op jit(solution)/shard_map/ppermute | solution.py:478
  49.4 6.8 %collective-permute-start.9 = (f32[64,256]{1,0:T(8,128)S(1)}, f32[64,256]{1,0:T(8,128)S(1)}, u32[]{:S(2)}, u32[]{:S(2)}) collective-permute-start(f32[64,256]{1,0:T(8,128)S(1)} %add.36), channel_id=1, source_target_pairs={{0,16},{4,20},{8,24},{12,28},{16,0},{20,4},{24,8},{28,12},{1,17},{... | collective-permute-start | bytes 196616 | tf_op jit(solution)/shard_map/ppermute | solution.py:478
  53.2 21.4 %collective-permute-start = (bf16[16,128,128]{2,1,0:T(8,128)(2,1)S(1)}, bf16[16,128,128]{2,1,0:T(8,128)(2,1)S(1)}, u32[]{:S(2)}, u32[]{:S(2)}) collective-permute-start(bf16[16,128,128]{2,1,0:T(8,128)(2,1)S(1)} %get-tuple-element.16), channel_id=1, source_target_pairs={{0,1},{1,0},{2,3},{3,2},{4,5},{5,4},{6,7},{7,6},{8,9},{9,8},{10,11... | collective-permute-start | bytes 1572872 | tf_op jit(solution)/shard_map/ppermute | solution.py:478
  53.2 4.3 %collective-permute-start.3 = (bf16[512,128]{1,0:T(8,128)(2,1)S(1)}, bf16[512,128]{1,0:T(8,128)(2,1)S(1)}, u32[]{:S(2)}, u32[]{:S(2)}) collective-permute-start(bf16[512,128]{1,0:T(8,128)(2,1)S(1)} %bitcast.18), channel_id=1, source_target_pairs={{0,1},{1,0},{2,3},{3,2},{4,5},{5,4},{6,7},{7,6},{8,9},{9,8},{10,11... | collective-permute-start | bytes 393224 | tf_op jit(solution)/shard_map/ppermute | solution.py:478
  56.2 3.5 %collective-permute-start.10 = (f32[64,256]{1,0:T(8,128)S(1)}, f32[64,256]{1,0:T(8,128)S(1)}, u32[]{:S(2)}, u32[]{:S(2)}) collective-permute-start(f32[64,256]{1,0:T(8,128)S(1)} %add.37), channel_id=1, source_target_pairs={{0,1},{1,0},{2,3},{3,2},{4,5},{5,4},{6,7},{7,6},{8,9},{9,8},{10,11... | collective-permute-start | bytes 196616 | tf_op jit(solution)/shard_map/ppermute | solution.py:478
  57.4 17.2 %collective-permute-start.2 = (bf16[16,128,128]{2,1,0:T(8,128)(2,1)S(1)}, bf16[16,128,128]{2,1,0:T(8,128)(2,1)S(1)}, u32[]{:S(2)}, u32[]{:S(2)}) collective-permute-start(bf16[16,128,128]{2,1,0:T(8,128)(2,1)S(1)} %add_convert_fusion), channel_id=1, source_target_pairs={{0,2},{1,3},{2,0},{3,1},{4,6},{5,7},{6,4},{7,5},{8,10},{9,11},{10,... | collective-permute-start | bytes 1572872 | tf_op jit(solution)/shard_map/ppermute | solution.py:478
  57.6 17.0 %collective-permute-start.4 = (bf16[512,128]{1,0:T(8,128)(2,1)S(1)}, bf16[512,128]{1,0:T(8,128)(2,1)S(1)}, u32[]{:S(2)}, u32[]{:S(2)}) collective-permute-start(bf16[512,128]{1,0:T(8,128)(2,1)S(1)} %add_convert_fusion.1.here), channel_id=1, source_target_pairs={{0,2},{1,3},{2,0},{3,1},{4,6},{5,7},{6,4},{7,5},{8,10},{9,11},{10,... | collective-permute-start | bytes 393224 | tf_op jit(solution)/shard_map/ppermute | solution.py:478

commit v2 on v1

--- a/solution.py
+++ b/solution.py
@@ -1,4 +1,5 @@
 import functools
+import math
 
 import jax
 import jax.numpy as jnp
@@ -11,7 +12,8 @@
 LANES = 128
 BITS_TILE, BITS_OTHER = 10, 7
 SIZE = 2
-UNROLL_FORWARD, UNROLL_HALO, UNROLL_BACKWARD = 36, 8, 36
+UNROLL_FORWARD, UNROLL_HALO, UNROLL_RETURN, UNROLL_BACKWARD = 36, 20, 16, 48
+WIDTH = 16
 PARTS = 8
 F32 = jnp.float32
 BF16 = jnp.bfloat16
@@ -300,7 +302,7 @@
     table, acc_in, halo, weight, out_grad_in, tiles, act, wgrad, back, sent_a, kept_a, sent_b, kept_b,
     held, some, rows, sums, hsum, lsum, grads, acc, out_grad, sems, few
 ):
-    _, tile, _ = tiles.shape
+    count, tile, _ = tiles.shape
     targets = acc.shape[0]
     halos = halo.shape[0] // tile
     ahead, order = plans(table, table.shape[1] // 2 - LANES)
@@ -313,7 +315,10 @@
 
     def fetch(n, carry):
         for i in range(batch):
-            t = jnp.maximum(tile_of(entry_of(n, i)), 1) - 1
+            slot = n * batch + i
+            real = SIZE * low + slot < SIZE * high
+            t = jnp.where(real, jnp.maximum(tile_of(entry_of(n, i)), 1) - 1, slot)
+            t = jnp.minimum(t, count - 1)
             pltpu.make_async_copy(tiles.at[t], some.at[n * batch + i], few.at[n]).start()
         return carry
 
@@ -349,7 +354,7 @@
     lax.fori_loop(0, groups, add, 0)
     wgrad[...] = jnp.zeros(wgrad.shape, F32)
     wait_all(inputs)
-    width = 4
+    width = math.gcd(targets, WIDTH)
 
     def dense(b, carry):
         many = []
@@ -373,7 +378,7 @@
     lax.fori_loop(0, targets // width, dense, 0)
     wait_all(large)
     product = scatter_product(held, grads)
-    run_sets(order, 0, halos, hsum, 0, UNROLL_HALO, product)
+    run_sets(order, 0, halos, hsum, 0, UNROLL_RETURN, product)
 
     def turn(s, carry):
         back[block(s, tile), :] = hsum[s].T.astype(BF16)
@@ -387,7 +392,7 @@
         sent_a[k] = lsum[k].astype(BF16)
         kept_a[k] = lsum[part + k]
         sent_b[k] = lsum[2 * part + k].astype(BF16)
-        kept_b[k] = lsum[3 * part + k]
+        kept_b[k] = lsum[3 * part + k].astype(BF16)
         return carry
 
     lax.fori_loop(0, part, flush, 0)
@@ -409,7 +414,7 @@
             jax.ShapeDtypeStruct((quarter, feat, tile), BF16),
             pltpu.VMEM((quarter, feat, tile), F32),
             jax.ShapeDtypeStruct((quarter, feat, tile), BF16),
-            pltpu.HBM((quarter, feat, tile), F32),
+            jax.ShapeDtypeStruct((quarter, feat, tile), BF16),
         ),
         in_specs=[SMEM, HBM, VMEM, VMEM, HBM, HBM],
         out_specs=(VMEM,) * 7,
@@ -435,43 +440,49 @@
     )(table, *in_hbm(acc), halo, weight, *in_hbm(out_grad, tiles))
 
 
-def finish_kernel(index, kept, near, far, here, there, out, both):
-    count, feat, tile = kept.shape
+def finish_kernel(mine, index, kept, near, far, here, there, out, rows):
+    count, _, tile = kept.shape
     base = lax.axis_index("rep") * (count * tile)
     slots = index.shape[1]
     sub = lax.broadcasted_iota(jnp.int32, (tile, slots), 0)
-    both[:, :feat] = here[...]
-    both[:, feat:] = there[...]
-    width = 4
+
+    @pl.when(mine[0] == 1)
+    def _():
+        rows[...] = here[...]
+
+    @pl.when(mine[0] == 0)
+    def _():
+        rows[...] = there[...]
+
+    width = math.gcd(count, WIDTH)
 
     def one(b, carry):
         for u in range(width):
             k = b * width + u
-            total = kept[k] + near[k].astype(F32) + far[k].astype(F32)
+            total = kept[k].astype(F32) + near[k].astype(F32) + far[k].astype(F32)
             hit = jnp.where(index[...] - (base + k * tile) == sub, 1.0, 0.0).astype(BF16)
-            extra = dot(hit, both[...])
-            out[block(k, tile), :] = (total.T + extra[:, :feat] + extra[:, feat:]).astype(BF16)
+            out[block(k, tile), :] = (total.T + dot(hit, rows[...])).astype(BF16)
         return carry
 
     lax.fori_loop(0, count // width, one, 0)
 
 
-def finish(index, kept, near, far, here, there):
+def finish(index, kept, near, far, here, there, mine):
     count, feat, tile = kept.shape
     return pl.pallas_call(
         finish_kernel,
         name="finish",
         out_shape=jax.ShapeDtypeStruct((count * tile, feat), BF16),
-        in_specs=[VMEM] * 6,
+        in_specs=[SMEM] + [VMEM] * 6,
         out_specs=VMEM,
-        scratch_shapes=[pltpu.VMEM((here.shape[0], 2 * feat), BF16)],
+        scratch_shapes=[pltpu.VMEM(here.shape, BF16)],
         compiler_params=pltpu.CompilerParams(vmem_limit_bytes=24 * MIB),
         cost_estimate=pl.CostEstimate(
             flops=4 * count * tile * feat * index.shape[1],
             bytes_accessed=kept.size * 10,
             transcendentals=0,
         ),
-    )(index, kept, near, far, here, there)
+    )(mine.astype(jnp.int32).reshape(1), index, kept, near, far, here, there)
 
 
 def swap(x, axis, size, bit):
@@ -527,24 +538,45 @@
     across = (kept_a + near_a.astype(F32)).astype(BF16)
     far = swap(across, "rep", n_rep, 2)
 
-    returned = exchange(back.reshape(n_dom, cap, feat)).reshape(-1, feat)
-    beside = swap(returned, "rep", n_rep, 1)
-    here = (returned.astype(F32) + beside.astype(F32)).astype(BF16)
-    there = swap(here, "rep", n_rep, 2)
+    back = back.reshape(2, n_dom // 2 * cap, feat)
+    hnear = swap(pick_one(back, 1 - low_bit), "rep", n_rep, 1)
+    hhalf = (pick_one(back, low_bit).astype(F32) + hnear.astype(F32)).astype(BF16)
+    hside = swap(hhalf, "rep", n_rep, 2)
+    hfull = (hhalf.astype(F32) + hside.astype(F32)).astype(BF16)
 
     halves = wpart.reshape(2, feat // 2, hidden)
     near = swap(pick_one(halves, 1 - low_bit), "rep", n_rep, 1)
     total = plus(pick_one(halves, low_bit), near)
     total = plus(total, swap(total, "rep", n_rep, 2))
-    bit = 1
-    while bit < n_dom:
+
+    here = lax.axis_index("dom")
+    blocks = hfull.reshape(1, n_dom // 2, cap, feat)
+    bit = n_dom // 2
+    while bit:
+        kept, sent = blocks, blocks
+        if bit < n_dom // 2:
+            split = blocks.reshape(blocks.shape[0], 2, -1, cap, feat)
+            own = jnp.minimum(here & bit, 1)
+            kept = lax.dynamic_index_in_dim(split, own, 1, False)
+            sent = lax.dynamic_index_in_dim(split, 1 - own, 1, False)
+        came = swap(sent, "dom", n_dom, bit)
+        blocks = jnp.concatenate([kept, came], axis=0)
         total = plus(total, swap(total, "dom", n_dom, bit))
-        bit *= 2
+        bit //= 2
+    arrived = blocks.reshape(-1, feat)
+    beside = swap(arrived, "rep", n_rep, 1)
     weight_grad = join(low_bit, total, swap(total, "rep", n_rep, 1))
+    mine = here // (n_dom // 2) == low_bit
 
     valid = jnp.arange(cap, dtype=jnp.int32)[None, :] < send_count[0][:, None]
-    index = jnp.where(valid, rows, -1).reshape(1, -1)
-    node_grad = finish(index, kept_b, near_b, far, here, there)
+    index = jnp.where(valid, rows, -1)
+    bits = n_dom.bit_length() - 1
+    index = index.reshape((2,) * bits + (cap,))
+    for axis in range(bits):
+        flip = (here >> (bits - 1 - axis)) & 1
+        index = jnp.where(flip == 1, jnp.flip(index, axis), index)
+    index = index.transpose(tuple(reversed(range(bits))) + (bits,)).reshape(1, -1)
+    node_grad = finish(index, kept_b, near_b, far, arrived, beside, mine)
     return (activated, node_grad, weight_grad)
 
 

time: 77.2 us -> 68.7 us (0.89)
  waiting for transfers between devices: 23.2 us -> 15.4 us
  Pallas kernels: 24.3 us -> 22.7 us
    ppermute x11 -> x15, waiting for transfers between devices: 23.2 us -> 15.4 us  [swap(): return lax.ppermute(x, axis, [(i, i ^ bit) for i in range(size)])]
    all_to_all x2 -> x1, starting transfers between devices: 13.5 us -> 7.29 us  [exchange(): return lax.all_to_all(x, 'dom', split_axis=0, concat_axis=0, tiled=True)]
    ppermute x11 -> x15, starting transfers between devices: 12.8 us -> 18.6 us  [swap(): return lax.ppermute(x, axis, [(i, i ^ bit) for i in range(size)])]
    pallas_call x1, Pallas kernels: 11.6 us -> 10.6 us  [middle(): pl.pallas_call(middle_kernel, name='middle', out_shape=(jax.ShapeDtypeStr...]
  transfers between devices with their start and end apart: 13 -> 16, of which waited for: 5 -> 7; matrix products, arithmetic and copies ran while one was open for 3% -> 5% of each run, Pallas kernels for 10% -> 11%
where the time goes in v2:
time: 68.7 us; the launch traced here: 68.4 us
  starting transfers between devices  25.9 us (38%)
  Pallas kernels  22.7 us (33%)
  waiting for transfers between devices  15.4 us (22%)
  other arithmetic  2.79 us (4%)
  local copies, waits for them, and re-layouts  0.85 us (1%)
  between operations  0.81 us (1%)
    ppermute x15, starting transfers between devices, swap(): return lax.ppermute(x, axis, [(i, i ^ bit) for i in range(size)])  18.6 us
    ppermute x15, waiting for transfers between devices, swap(): return lax.ppermute(x, axis, [(i, i ^ bit) for i in range(size)])  15.4 us
    pallas_call x1, Pallas kernels, middle(): pl.pallas_call(middle_kernel, name='middle', out_shape=(jax.ShapeDtypeStr...  10.6 us
    pallas_call x1, Pallas kernels, forward(): pl.pallas_call(functools.partial(forward_kernel, ranks, halos), name='for...  7.5 us
    all_to_all x1, starting transfers between devices, exchange(): return lax.all_to_all(x, 'dom', split_axis=0, concat_axis=0, tiled=True)  7.29 us
    pallas_call x1, Pallas kernels, pick(): pl.pallas_call(pick_kernel, name='pick', out_shape=jax.ShapeDtypeStruct((...  3.07 us
    pallas_call x1, Pallas kernels, finish(): pl.pallas_call(finish_kernel, name='finish', out_shape=jax.ShapeDtypeStru...  1.54 us
  transfers between devices with their start and end apart: 16, of which 7 were waited for; matrix products, arithmetic and copies ran while one was open for 5% of the time, Pallas kernels for 11%

profile of v2, /device:TPU:0, one launch (start us, length us, event | category | flops | bytes accessed | tf_op | source)
XLA Modules:
  0.0 68.4 jit_solution(12783553795099650104)
XLA Ops:
  0.6 0.0 copy-start.1
  0.6 0.0 copy-start.2
  0.7 3.1 %pick.1 = bf16[512,128]{1,0:T(8,128)(2,1)} custom-call(s32[8,64]{1,0:T(8,128)} %bitcast.41, s32[1,8]{1,0:T(1,128)} %counts_in.1, bf16[8192,128]{1,0:T(8,128)(2,1)} %feat_in.3), custom_call_target="tpu_custom_call" | custom-call | flops 1048576 | bytes 4194304 | tf_op jit(solution)/shard_map/pick/pallas_call | solution.py:87
  3.7 7.3 %all-to-all-start = ((bf16[8,64,128]{2,1,0:T(8,128)(2,1)}), bf16[8,64,128]{2,1,0:T(8,128)(2,1)S(1)}, u32[]{:S(2)}, u32[]{:S(2)}) async-start(bf16[8,64,128]{2,1,0:T(8,128)(2,1)} %bitcast.4), calls=%async_computation | async-start | bytes 262144 | tf_op jit(solution)/shard_map/all_to_all | solution.py:497
  11.0 0.5 broadcast.10
  11.5 0.0 copy-done.2
  11.5 0.7 reduce.3
  12.2 0.1 lt.41
  12.3 0.1 copy.11
  12.4 0.0 copy-done.1
  12.4 0.1 compare_select_fusion
  12.5 0.0 copy-start
  12.5 7.5 %forward.1 = (f32[17,128,128]{2,1,0:T(8,128)}, s32[1,1024]{1,0:T(1,128)S(1)}) custom-call(s32[1,256]{1,0:T(1,128)} %bitcast.46, s32[1,256]{1,0:T(1,128)} %bitcast.47, bf16[8192,128]{1,0:T(8,128)(2,1)} %feat_in.3, bf16[256,128,128]{2,1,0:T(8,128)(2,1)} %bitcast.44), custom_call_target="tpu_custom_call" | custom-call | flops 4294967296 | bytes 8388608 | tf_op jit(solution)/shard_map/forward/pallas_call | solution.py:277
  20.0 0.0 all-to-all-done
  20.0 0.0 copy-done
  20.0 10.6 %middle.1 = (bf16[2048,256]{1,0:T(8,128)(2,1)}, f32[128,256]{1,0:T(8,128)S(1)}, bf16[512,128]{1,0:T(8,128)(2,1)S(1)}, bf16[16,128,128]{2,1,0:T(8,128)(2,1)S(1)},...) custom-call(s32[1,1024]{1,0:T(1,128)S(1)} %get-tuple-element.12.table, ...), custom_call_target="tpu_custom_call" | custom-call | flops 5100273664 | bytes 4194304 | tf_op jit(solution)/shard_map/middle/pallas_call | solution.py:407
  30.7 0.1 collective-permute-start.1
  30.8 0.5 collective-permute-start.3
  31.3 0.1 collective-permute-start.9
  31.4 1.4 %collective-permute-done.3 = bf16[256,128]{1,0:T(8,128)(2,1)S(1)} collective-permute-done((bf16[256,128]{1,0:T(8,128)(2,1)S(1)}, bf16[256,128]{1,0:T(8,128)(2,1)S(1)}, u32[]{:S(2)}, u32[]{:S(2)}) %collective-permute-start.3) | collective-permute-done | bytes 65568 | tf_op jit(solution)/shard_map/ppermute | solution.py:489
  32.8 1.6 %collective-permute-start.4 = (bf16[256,128]{1,0:T(8,128)(2,1)S(1)}, bf16[256,128]{1,0:T(8,128)(2,1)S(1)}, u32[]{:S(2)}, u32[]{:S(2)}) collective-permute-start(bf16[256,128]{1,0:T(8,128)(2,1)S(1)} %fusion), channel_id=1, source_target_pairs={{0,2},{1,3},{2,0},{3,1},{4,6},{5,7},{6,4},{7,5},{8,10},{9,11},{10,... | collective-permute-start | bytes 196616 | tf_op jit(solution)/shard_map/ppermute | solution.py:489
  34.4 0.0 collective-permute-done.9
  34.4 0.5 collective-permute-start.10
  35.0 2.3 %collective-permute-done.4 = bf16[256,128]{1,0:T(8,128)(2,1)S(1)} collective-permute-done((bf16[256,128]{1,0:T(8,128)(2,1)S(1)}, bf16[256,128]{1,0:T(8,128)(2,1)S(1)}, u32[]{:S(2)}, u32[]{:S(2)}) %collective-permute-start.4) | collective-permute-done | bytes 65568 | tf_op jit(solution)/shard_map/ppermute | solution.py:489
  37.3 3.1 %collective-permute-start.5 = (bf16[1,4,64,128]{3,2,1,0:T(8,128)(2,1)S(1)}, bf16[1,4,64,128]{3,2,1,0:T(8,128)(2,1)S(1)}, u32[]{:S(2)}, u32[]{:S(2)}) collective-permute-start(bf16[1,4,64,128]{3,2,1,0:T(8,128)(2,1)S(1)} %bitcast.38), channel_id=1, source_target_pairs={{0,16},{4,20},{8,24},{12,28},{16,0},{20,4},{24,8},{28,12},{1,17},{... | collective-permute-start | bytes 196616 | tf_op jit(solution)/shard_map/ppermute | solution.py:489
  40.4 0.1 broadcast_select_fusion.2
  40.5 0.0 collective-permute-done.10
  40.5 1.3 %collective-permute-start.11 = (f32[64,256]{1,0:T(8,128)S(1)}, f32[64,256]{1,0:T(8,128)S(1)}, u32[]{:S(2)}, u32[]{:S(2)}) collective-permute-start(f32[64,256]{1,0:T(8,128)S(1)} %add.62), channel_id=1, source_target_pairs={{0,16},{4,20},{8,24},{12,28},{16,0},{20,4},{24,8},{28,12},{1,17},{... | collective-permute-start | bytes 196616 | tf_op jit(solution)/shard_map/ppermute | solution.py:489
  41.8 1.0 %collective-permute-done.5 = bf16[1,4,64,128]{3,2,1,0:T(8,128)(2,1)S(1)} collective-permute-done((bf16[1,4,64,128]{3,2,1,0:T(8,128)(2,1)S(1)}, bf16[1,4,64,128]{3,2,1,0:T(8,128)(2,1)S(1)}, u32[]{:S(2)}, u32[]{:S(2)}) %collective-permute-start.5) | collective-permute-done | bytes 65568 | tf_op jit(solution)/shard_map/ppermute | solution.py:489
  42.8 3.1 %collective-permute-start.6 = (bf16[2,2,64,128]{3,2,0,1:T(8,128)(2,1)S(1)}, bf16[2,2,64,128]{3,2,0,1:T(8,128)(2,1)S(1)}, u32[]{:S(2)}, u32[]{:S(2)}) collective-permute-start(bf16[2,2,64,128]{3,2,0,1:T(8,128)(2,1)S(1)} %get-tuple-element.25), channel_id=1, source_target_pairs={{0,8},{4,12},{8,0},{12,4},{16,24},{20,28},{24,16},{28,20},{1,9},{5... | collective-permute-start | bytes 196616 | tf_op jit(solution)/shard_map/ppermute | solution.py:489
  45.9 0.0 collective-permute-start
  45.9 0.0 collective-permute-done.11
  45.9 1.8 %collective-permute-start.12 = (f32[64,256]{1,0:T(8,128)S(1)}, f32[64,256]{1,0:T(8,128)S(1)}, u32[]{:S(2)}, u32[]{:S(2)}) collective-permute-start(f32[64,256]{1,0:T(8,128)S(1)} %add.63), channel_id=1, source_target_pairs={{0,8},{4,12},{8,0},{12,4},{16,24},{20,28},{24,16},{28,20},{1,9},{5... | collective-permute-start | bytes 196616 | tf_op jit(solution)/shard_map/ppermute | solution.py:489
  47.7 0.5 collective-permute-done.6
  48.3 3.2 %collective-permute-start.7 = (bf16[4,1,64,128]{3,2,0,1:T(8,128)(2,1)S(1)}, bf16[4,1,64,128]{3,2,0,1:T(8,128)(2,1)S(1)}, u32[]{:S(2)}, u32[]{:S(2)}) collective-permute-start(bf16[4,1,64,128]{3,2,0,1:T(8,128)(2,1)S(1)} %get-tuple-element.24), channel_id=1, source_target_pairs={{0,4},{4,0},{8,12},{12,8},{16,20},{20,16},{24,28},{28,24},{1,5},{5... | collective-permute-start | bytes 196616 | tf_op jit(solution)/shard_map/ppermute | solution.py:489
  51.5 0.0 collective-permute-done.12
  51.5 0.9 %collective-permute-start.13 = (f32[64,256]{1,0:T(8,128)S(1)}, f32[64,256]{1,0:T(8,128)S(1)}, u32[]{:S(2)}, u32[]{:S(2)}) collective-permute-start(f32[64,256]{1,0:T(8,128)S(1)} %add.64), channel_id=1, source_target_pairs={{0,4},{4,0},{8,12},{12,8},{16,20},{20,16},{24,28},{28,24},{1,5},{5... | collective-permute-start | bytes 196616 | tf_op jit(solution)/shard_map/ppermute | solution.py:489
  52.5 0.0 collective-permute-done.1
  52.5 1.2 %add_convert_fusion = bf16[16,128,128]{2,1,0:T(8,128)(2,1)S(1)} fusion(f32[16,128,128]{2,1,0:T(8,128)S(1)} %get-tuple-element.17, bf16[16,128,128]{2,1,0:T(8,128)(2,1)} %collective-permute-done.1), kind=kLoop, calls=%fused_computation | loop fusion | flops 786432 | bytes 2097152 | tf_op jit(solution)/shard_map/convert_element_type | solution.py:538
  53.6 1.7 %collective-permute-start.2 = (bf16[16,128,128]{2,1,0:T(8,128)(2,1)S(1)}, bf16[16,128,128]{2,1,0:T(8,128)(2,1)S(1)}, u32[]{:S(2)}, u32[]{:S(2)}) collective-permute-start(bf16[16,128,128]{2,1,0:T(8,128)(2,1)S(1)} %add_convert_fusion), channel_id=1, source_target_pairs={{0,2},{1,3},{2,0},{3,1},{4,6},{5,7},{6,4},{7,5},{8,10},{9,11},{10,... | collective-permute-start | bytes 1572872 | tf_op jit(solution)/shard_map/ppermute | solution.py:489
  55.4 0.1 reshape.58.index
  55.5 0.4 collective-permute-done.13
  55.9 0.1 collective-permute-start.14
  56.0 0.0 collective-permute-done.7
  56.0 0.5 collective-permute-start.8
  56.6 0.7 collective-permute-done.14
  57.2 0.7 pad_maximum_fusion.1
  57.9 0.0 collective-permute-done.8.there
  57.9 0.0 collective-permute-done.near
  57.9 9.0 %collective-permute-done.2.far = bf16[16,128,128]{2,1,0:T(8,128)(2,1)S(1)} collective-permute-done((bf16[16,128,128]{2,1,0:T(8,128)(2,1)S(1)}, bf16[16,128,128]{2,1,0:T(8,128)(2,1)S(1)}, u32[]{:S(2)}, u32[]{:S(2)}) %collective-permute-start.2) | collective-permute-done | bytes 524320 | tf_op jit(solution)/shard_map/ppermute | solution.py:489
  66.9 1.5 %finish.1 = bf16[2048,128]{1,0:T(8,128)(2,1)} custom-call(s32[1]{0:T(128)} %bitcast.6.mine, s32[1,512]{1,0:T(1,128)S(1)} %reshape.58.index, bf16[16,128,128]{2,1,0:T(8,128)(2,1)S(1)} %get-tuple-element.15.kept, bf16[16,128,128]{2,1,0:T(8,128)(2,1)S(1)} %collective-permute-done.near, bf16[16,128,128]{2,1,0:T(8,128)(2,1)S(1)} %collective-permute-done.2.far, ...), custom_call_target="tpu_custom_call" | custom-call | flops 536870912 | bytes 2621440 | tf_op jit(solution)/shard_map/finish/pallas_call | solution.py:472
  (16 shorter events, 0.2 us)
Async XLA Ops:
  0.6 11.8 %copy-start.1 = (s32[1,8,64]{2,1,0:T(8,128)S(1)}, s32[1,8,64]{2,1,0:T(8,128)}, u32[]{:S(2)}) copy-start(s32[1,8,64]{2,1,0:T(8,128)} %param.11) | copy-start | bytes 6148
  0.6 10.9 %copy-start.2 = (s32[1,8]{1,0:T(1,128)S(1)}, s32[1,8]{1,0:T(1,128)}, u32[]{:S(2)}) copy-start(s32[1,8]{1,0:T(1,128)} %counts_in.1) | copy-start | bytes 100
  3.7 16.3 %all-to-all-start = ((bf16[8,64,128]{2,1,0:T(8,128)(2,1)}), bf16[8,64,128]{2,1,0:T(8,128)(2,1)S(1)}, u32[]{:S(2)}, u32[]{:S(2)}) async-start(bf16[8,64,128]{2,1,0:T(8,128)(2,1)} %bitcast.4), calls=%async_computation | async-start | bytes 262144 | tf_op jit(solution)/shard_map/all_to_all | solution.py:497
  12.5 7.5 %copy-start = (bf16[128,256]{1,0:T(8,128)(2,1)S(1)}, bf16[128,256]{1,0:T(8,128)(2,1)}, u32[]{:S(2)}) copy-start(bf16[128,256]{1,0:T(8,128)(2,1)} %weight.1) | copy-start | bytes 196612
  30.7 21.8 %collective-permute-start.1 = (bf16[16,128,128]{2,1,0:T(8,128)(2,1)S(1)}, bf16[16,128,128]{2,1,0:T(8,128)(2,1)}, u32[]{:S(2)}, u32[]{:S(2)}) collective-permute-start(bf16[16,128,128]{2,1,0:T(8,128)(2,1)S(1)} %get-tuple-element.18), channel_id=1, source_target_pairs={{0,1},{1,0},{2,3},{3,2},{4,5},{5,4},{6,7},{7,6},{8,9},{9,8},{10,11... | collective-permute-start | bytes 1572872 | tf_op jit(solution)/shard_map/ppermute | solution.py:489
  30.8 2.0 %collective-permute-start.3 = (bf16[256,128]{1,0:T(8,128)(2,1)S(1)}, bf16[256,128]{1,0:T(8,128)(2,1)S(1)}, u32[]{:S(2)}, u32[]{:S(2)}) collective-permute-start(bf16[256,128]{1,0:T(8,128)(2,1)S(1)} %dynamic-slice_bitcast_fusion.1), channel_id=1, source_target_pairs={{0,1},{1,0},{2,3},{3,2},{4,5},{5,4},{6,7},{7,6},{8,9},{9,8},{10,11... | collective-permute-start | bytes 196616 | tf_op jit(solution)/shard_map/ppermute | solution.py:489
  31.3 3.2 %collective-permute-start.9 = (f32[64,256]{1,0:T(8,128)S(1)}, f32[64,256]{1,0:T(8,128)S(1)}, u32[]{:S(2)}, u32[]{:S(2)}) collective-permute-start(f32[64,256]{1,0:T(8,128)S(1)} %dynamic-slice_bitcast_fusion), channel_id=1, source_target_pairs={{0,1},{1,0},{2,3},{3,2},{4,5},{5,4},{6,7},{7,6},{8,9},{9,8},{10,11... | collective-permute-start | bytes 196616 | tf_op jit(solution)/shard_map/ppermute | solution.py:489
  32.8 4.5 %collective-permute-start.4 = (bf16[256,128]{1,0:T(8,128)(2,1)S(1)}, bf16[256,128]{1,0:T(8,128)(2,1)S(1)}, u32[]{:S(2)}, u32[]{:S(2)}) collective-permute-start(bf16[256,128]{1,0:T(8,128)(2,1)S(1)} %fusion), channel_id=1, source_target_pairs={{0,2},{1,3},{2,0},{3,1},{4,6},{5,7},{6,4},{7,5},{8,10},{9,11},{10,... | collective-permute-start | bytes 196616 | tf_op jit(solution)/shard_map/ppermute | solution.py:489
  34.4 6.0 %collective-permute-start.10 = (f32[64,256]{1,0:T(8,128)S(1)}, f32[64,256]{1,0:T(8,128)S(1)}, u32[]{:S(2)}, u32[]{:S(2)}) collective-permute-start(f32[64,256]{1,0:T(8,128)S(1)} %bitcast_add_fusion), channel_id=1, source_target_pairs={{0,2},{1,3},{2,0},{3,1},{4,6},{5,7},{6,4},{7,5},{8,10},{9,11},{10,... | collective-permute-start | bytes 196616 | tf_op jit(solution)/shard_map/ppermute | solution.py:489
  37.3 5.4 %collective-permute-start.5 = (bf16[1,4,64,128]{3,2,1,0:T(8,128)(2,1)S(1)}, bf16[1,4,64,128]{3,2,1,0:T(8,128)(2,1)S(1)}, u32[]{:S(2)}, u32[]{:S(2)}) collective-permute-start(bf16[1,4,64,128]{3,2,1,0:T(8,128)(2,1)S(1)} %bitcast.38), channel_id=1, source_target_pairs={{0,16},{4,20},{8,24},{12,28},{16,0},{20,4},{24,8},{28,12},{1,17},{... | collective-permute-start | bytes 196616 | tf_op jit(solution)/shard_map/ppermute | solution.py:489
  40.5 5.4 %collective-permute-start.11 = (f32[64,256]{1,0:T(8,128)S(1)}, f32[64,256]{1,0:T(8,128)S(1)}, u32[]{:S(2)}, u32[]{:S(2)}) collective-permute-start(f32[64,256]{1,0:T(8,128)S(1)} %add.62), channel_id=1, source_target_pairs={{0,16},{4,20},{8,24},{12,28},{16,0},{20,4},{24,8},{28,12},{1,17},{... | collective-permute-start | bytes 196616 | tf_op jit(solution)/shard_map/ppermute | solution.py:489
  42.8 5.5 %collective-permute-start.6 = (bf16[2,2,64,128]{3,2,0,1:T(8,128)(2,1)S(1)}, bf16[2,2,64,128]{3,2,0,1:T(8,128)(2,1)S(1)}, u32[]{:S(2)}, u32[]{:S(2)}) collective-permute-start(bf16[2,2,64,128]{3,2,0,1:T(8,128)(2,1)S(1)} %get-tuple-element.25), channel_id=1, source_target_pairs={{0,8},{4,12},{8,0},{12,4},{16,24},{20,28},{24,16},{28,20},{1,9},{5... | collective-permute-start | bytes 196616 | tf_op jit(solution)/shard_map/ppermute | solution.py:489
  45.9 12.0 %collective-permute-start = (bf16[16,128,128]{2,1,0:T(8,128)(2,1)S(1)}, bf16[16,128,128]{2,1,0:T(8,128)(2,1)S(1)}, u32[]{:S(2)}, u32[]{:S(2)}) collective-permute-start(bf16[16,128,128]{2,1,0:T(8,128)(2,1)S(1)} %get-tuple-element.16), channel_id=1, source_target_pairs={{0,1},{1,0},{2,3},{3,2},{4,5},{5,4},{6,7},{7,6},{8,9},{9,8},{10,11... | collective-permute-start | bytes 1572872 | tf_op jit(solution)/shard_map/ppermute | solution.py:489
  45.9 5.6 %collective-permute-start.12 = (f32[64,256]{1,0:T(8,128)S(1)}, f32[64,256]{1,0:T(8,128)S(1)}, u32[]{:S(2)}, u32[]{:S(2)}) collective-permute-start(f32[64,256]{1,0:T(8,128)S(1)} %add.63), channel_id=1, source_target_pairs={{0,8},{4,12},{8,0},{12,4},{16,24},{20,28},{24,16},{28,20},{1,9},{5... | collective-permute-start | bytes 196616 | tf_op jit(solution)/shard_map/ppermute | solution.py:489
  48.3 7.7 %collective-permute-start.7 = (bf16[4,1,64,128]{3,2,0,1:T(8,128)(2,1)S(1)}, bf16[4,1,64,128]{3,2,0,1:T(8,128)(2,1)S(1)}, u32[]{:S(2)}, u32[]{:S(2)}) collective-permute-start(bf16[4,1,64,128]{3,2,0,1:T(8,128)(2,1)S(1)} %get-tuple-element.24), channel_id=1, source_target_pairs={{0,4},{4,0},{8,12},{12,8},{16,20},{20,16},{24,28},{28,24},{1,5},{5... | collective-permute-start | bytes 196616 | tf_op jit(solution)/shard_map/ppermute | solution.py:489
  51.5 4.3 %collective-permute-start.13 = (f32[64,256]{1,0:T(8,128)S(1)}, f32[64,256]{1,0:T(8,128)S(1)}, u32[]{:S(2)}, u32[]{:S(2)}) collective-permute-start(f32[64,256]{1,0:T(8,128)S(1)} %add.64), channel_id=1, source_target_pairs={{0,4},{4,0},{8,12},{12,8},{16,20},{20,16},{24,28},{28,24},{1,5},{5... | collective-permute-start | bytes 196616 | tf_op jit(solution)/shard_map/ppermute | solution.py:489
  53.6 13.3 %collective-permute-start.2 = (bf16[16,128,128]{2,1,0:T(8,128)(2,1)S(1)}, bf16[16,128,128]{2,1,0:T(8,128)(2,1)S(1)}, u32[]{:S(2)}, u32[]{:S(2)}) collective-permute-start(bf16[16,128,128]{2,1,0:T(8,128)(2,1)S(1)} %add_convert_fusion), channel_id=1, source_target_pairs={{0,2},{1,3},{2,0},{3,1},{4,6},{5,7},{6,4},{7,5},{8,10},{9,11},{10,... | collective-permute-start | bytes 1572872 | tf_op jit(solution)/shard_map/ppermute | solution.py:489
  55.9 1.3 %collective-permute-start.14 = (f32[64,256]{1,0:T(8,128)S(1)}, f32[64,256]{1,0:T(8,128)S(1)}, u32[]{:S(2)}, u32[]{:S(2)}) collective-permute-start(f32[64,256]{1,0:T(8,128)S(1)} %add.65), channel_id=1, source_target_pairs={{0,1},{1,0},{2,3},{3,2},{4,5},{5,4},{6,7},{7,6},{8,9},{9,8},{10,11... | collective-permute-start | bytes 196616 | tf_op jit(solution)/shard_map/ppermute | solution.py:489
  56.0 1.9 %collective-permute-start.8 = (bf16[512,128]{1,0:T(8,128)(2,1)S(1)}, bf16[512,128]{1,0:T(8,128)(2,1)S(1)}, u32[]{:S(2)}, u32[]{:S(2)}) collective-permute-start(bf16[512,128]{1,0:T(8,128)(2,1)S(1)} %bitcast.31), channel_id=1, source_target_pairs={{0,1},{1,0},{2,3},{3,2},{4,5},{5,4},{6,7},{7,6},{8,9},{9,8},{10,11... | collective-permute-start | bytes 393224 | tf_op jit(solution)/shard_map/ppermute | solution.py:489

commit v3 on v2

--- a/solution.py
+++ b/solution.py
@@ -390,7 +390,7 @@
 
     def flush(k, carry):
         sent_a[k] = lsum[k].astype(BF16)
-        kept_a[k] = lsum[part + k]
+        kept_a[k] = lsum[part + k].astype(BF16)
         sent_b[k] = lsum[2 * part + k].astype(BF16)
         kept_b[k] = lsum[3 * part + k].astype(BF16)
         return carry
@@ -412,7 +412,7 @@
             jax.ShapeDtypeStruct((feat, hidden), F32),
             jax.ShapeDtypeStruct(halo.shape, BF16),
             jax.ShapeDtypeStruct((quarter, feat, tile), BF16),
-            pltpu.VMEM((quarter, feat, tile), F32),
+            pltpu.VMEM((quarter, feat, tile), BF16),
             jax.ShapeDtypeStruct((quarter, feat, tile), BF16),
             jax.ShapeDtypeStruct((quarter, feat, tile), BF16),
         ),
@@ -535,7 +535,7 @@
 
     near_a = swap(sent_a, "rep", n_rep, 1)
     near_b = swap(sent_b, "rep", n_rep, 1)
-    across = (kept_a + near_a.astype(F32)).astype(BF16)
+    across = (kept_a.astype(F32) + near_a.astype(F32)).astype(BF16)
     far = swap(across, "rep", n_rep, 2)
 
     back = back.reshape(2, n_dom // 2 * cap, feat)
@@ -561,7 +561,9 @@
             sent = lax.dynamic_index_in_dim(split, 1 - own, 1, False)
         came = swap(sent, "dom", n_dom, bit)
         blocks = jnp.concatenate([kept, came], axis=0)
-        total = plus(total, swap(total, "dom", n_dom, bit))
+        total = lax.reduce_precision(total, 8, 7)
+        got = swap(total.astype(BF16), "dom", n_dom, bit).astype(F32)
+        total = plus(total, got)
         bit //= 2
     arrived = blocks.reshape(-1, feat)
     beside = swap(arrived, "rep", n_rep, 1)

time: 68.7 us -> 65.7 us (0.956)
  starting transfers between devices: 25.9 us -> 24 us
  other arithmetic: 2.79 us -> 1.8 us
    ppermute x15, starting transfers between devices: 18.6 us -> 16.7 us  [swap(): return lax.ppermute(x, axis, [(i, i ^ bit) for i in range(size)])]
    convert_element_type x1 -> x4, other arithmetic: 1.17 us -> 0.19 us  [the longest x1 0.15 us: shards(): across = (kept_a.astype(F32) + near_a.astype(F32)).astype(BF16)]
  transfers between devices with their start and end apart: 16 -> 16, of which waited for: 7 -> 9; matrix products, arithmetic and copies ran while one was open for 5% -> 4% of each run, Pallas kernels for 11% -> 11%
where the time goes in v3:
time: 65.7 us; the launch traced here: 65.4 us
  starting transfers between devices  24 us (37%)
  Pallas kernels  22.7 us (35%)
  waiting for transfers between devices  15.2 us (23%)
  other arithmetic  1.8 us (3%)
  local copies, waits for them, and re-layouts  0.84 us (1%)
  between operations  0.78 us (1%)
    ppermute x15, starting transfers between devices, swap(): return lax.ppermute(x, axis, [(i, i ^ bit) for i in range(size)])  16.7 us
    ppermute x15, waiting for transfers between devices, swap(): return lax.ppermute(x, axis, [(i, i ^ bit) for i in range(size)])  15.2 us
    pallas_call x1, Pallas kernels, middle(): pl.pallas_call(middle_kernel, name='middle', out_shape=(jax.ShapeDtypeStr...  10.6 us
    pallas_call x1, Pallas kernels, forward(): pl.pallas_call(functools.partial(forward_kernel, ranks, halos), name='for...  7.49 us
    all_to_all x1, starting transfers between devices, exchange(): return lax.all_to_all(x, 'dom', split_axis=0, concat_axis=0, tiled=True)  7.29 us
    pallas_call x1, Pallas kernels, pick(): pl.pallas_call(pick_kernel, name='pick', out_shape=jax.ShapeDtypeStruct((...  3.07 us
    pallas_call x1, Pallas kernels, finish(): pl.pallas_call(finish_kernel, name='finish', out_shape=jax.ShapeDtypeStru...  1.56 us
  transfers between devices with their start and end apart: 16, of which 9 were waited for; matrix products, arithmetic and copies ran while one was open for 4% of the time, Pallas kernels for 11%

profile of v3, /device:TPU:0, one launch (start us, length us, event | category | flops | bytes accessed | tf_op | source)
XLA Modules:
  0.0 65.4 jit_solution(12416857540610581261)
XLA Ops:
  0.6 0.0 copy-start.1
  0.6 0.0 copy-start.2
  0.7 3.1 %pick.1 = bf16[512,128]{1,0:T(8,128)(2,1)} custom-call(s32[8,64]{1,0:T(8,128)} %bitcast.41, s32[1,8]{1,0:T(1,128)} %counts_in.1, bf16[8192,128]{1,0:T(8,128)(2,1)} %feat_in.3), custom_call_target="tpu_custom_call" | custom-call | flops 1048576 | bytes 4194304 | tf_op jit(solution)/shard_map/pick/pallas_call | solution.py:87
  3.7 7.3 %all-to-all-start = ((bf16[8,64,128]{2,1,0:T(8,128)(2,1)}), bf16[8,64,128]{2,1,0:T(8,128)(2,1)S(1)}, u32[]{:S(2)}, u32[]{:S(2)}) async-start(bf16[8,64,128]{2,1,0:T(8,128)(2,1)} %bitcast.4), calls=%async_computation | async-start | bytes 262144 | tf_op jit(solution)/shard_map/all_to_all | solution.py:497
  11.0 0.5 broadcast.10
  11.5 0.0 copy-done.2
  11.5 0.7 %reduce.3 = s32[8]{0:T(128)S(1)} reduce(s32[1,8]{1,0:T(1,128)S(1)} %copy-done.2, s32[]{:T(128)} %broadcast.10), dimensions={0}, to_apply=%param.12.reduce_sub_computation.3 | reduce | bytes 68 | tf_op args[4]
  12.2 0.1 lt.41
  12.3 0.1 copy.11
  12.4 0.0 copy-done.1
  12.4 0.1 compare_select_fusion
  12.5 0.1 broadcast_select_fusion.2
  12.6 0.1 reshape.58.index
  12.7 0.0 copy-start
  12.7 7.5 %forward.1 = (f32[17,128,128]{2,1,0:T(8,128)}, s32[1,1024]{1,0:T(1,128)S(1)}) custom-call(s32[1,256]{1,0:T(1,128)} %bitcast.46, s32[1,256]{1,0:T(1,128)} %bitcast.47, bf16[8192,128]{1,0:T(8,128)(2,1)} %feat_in.3, bf16[256,128,128]{2,1,0:T(8,128)(2,1)} %bitcast.44), custom_call_target="tpu_custom_call" | custom-call | flops 4294967296 | bytes 8388608 | tf_op jit(solution)/shard_map/forward/pallas_call | solution.py:277
  20.2 0.0 all-to-all-done
  20.2 0.0 copy-done
  20.2 10.6 %middle.1 = (bf16[2048,256]{1,0:T(8,128)(2,1)}, f32[128,256]{1,0:T(8,128)S(1)}, bf16[512,128]{1,0:T(8,128)(2,1)S(1)}, bf16[16,128,128]{2,1,0:T(8,128)(2,1)S(1)},...) custom-call(s32[1,1024]{1,0:T(1,128)S(1)} %get-tuple-element.12.table, ...), custom_call_target="tpu_custom_call" | custom-call | flops 5100273664 | bytes 4194304 | tf_op jit(solution)/shard_map/middle/pallas_call | solution.py:407
  30.8 0.1 collective-permute-start
  30.9 0.5 collective-permute-start.1
  31.4 0.1 collective-permute-start.9
  31.5 0.4 collective-permute-start.3
  31.9 1.7 %collective-permute-done.9 = f32[64,256]{1,0:T(8,128)S(1)} collective-permute-done((f32[64,256]{1,0:T(8,128)S(1)}, f32[64,256]{1,0:T(8,128)S(1)}, u32[]{:S(2)}, u32[]{:S(2)}) %collective-permute-start.9) | collective-permute-done | bytes 65568 | tf_op jit(solution)/shard_map/ppermute | solution.py:489
  33.7 1.6 %collective-permute-start.10 = (f32[64,256]{1,0:T(8,128)S(1)}, f32[64,256]{1,0:T(8,128)S(1)}, u32[]{:S(2)}, u32[]{:S(2)}) collective-permute-start(f32[64,256]{1,0:T(8,128)S(1)} %bitcast_add_fusion), channel_id=1, source_target_pairs={{0,2},{1,3},{2,0},{3,1},{4,6},{5,7},{6,4},{7,5},{8,10},{9,11},{10,... | collective-permute-start | bytes 196616 | tf_op jit(solution)/shard_map/ppermute | solution.py:489
  35.3 0.0 collective-permute-done.3
  35.3 0.5 collective-permute-start.4
  35.8 2.3 %collective-permute-done.10 = f32[64,256]{1,0:T(8,128)S(1)} collective-permute-done((f32[64,256]{1,0:T(8,128)S(1)}, f32[64,256]{1,0:T(8,128)S(1)}, u32[]{:S(2)}, u32[]{:S(2)}) %collective-permute-start.10) | collective-permute-done | bytes 65568 | tf_op jit(solution)/shard_map/ppermute | solution.py:489
  38.2 3.1 %collective-permute-start.11 = (bf16[64,256]{1,0:T(8,128)(2,1)S(1)}, bf16[64,256]{1,0:T(8,128)(2,1)S(1)}, u32[]{:S(2)}, u32[]{:S(2)}) collective-permute-start(bf16[64,256]{1,0:T(8,128)(2,1)S(1)} %get-tuple-element.21), channel_id=1, source_target_pairs={{0,16},{4,20},{8,24},{12,28},{16,0},{20,4},{24,8},{28,12},{1,17},{... | collective-permute-start | bytes 98312 | tf_op jit(solution)/shard_map/ppermute | solution.py:489
  41.2 0.0 collective-permute-done.4
  41.3 1.4 %collective-permute-start.5 = (bf16[1,4,64,128]{3,2,1,0:T(8,128)(2,1)S(1)}, bf16[1,4,64,128]{3,2,1,0:T(8,128)(2,1)S(1)}, u32[]{:S(2)}, u32[]{:S(2)}) collective-permute-start(bf16[1,4,64,128]{3,2,1,0:T(8,128)(2,1)S(1)} %bitcast.38), channel_id=1, source_target_pairs={{0,16},{4,20},{8,24},{12,28},{16,0},{20,4},{24,8},{28,12},{1,17},{... | collective-permute-start | bytes 196616 | tf_op jit(solution)/shard_map/ppermute | solution.py:489
  42.6 0.5 collective-permute-done.11
  43.1 2.4 %collective-permute-start.12 = (bf16[64,256]{1,0:T(8,128)(2,1)S(1)}, bf16[64,256]{1,0:T(8,128)(2,1)S(1)}, u32[]{:S(2)}, u32[]{:S(2)}) collective-permute-start(bf16[64,256]{1,0:T(8,128)(2,1)S(1)} %fusion.7), channel_id=1, source_target_pairs={{0,8},{4,12},{8,0},{12,4},{16,24},{20,28},{24,16},{28,20},{1,9},{5... | collective-permute-start | bytes 98312 | tf_op jit(solution)/shard_map/ppermute | solution.py:489
  45.5 1.0 %collective-permute-done.5 = bf16[1,4,64,128]{3,2,1,0:T(8,128)(2,1)S(1)} collective-permute-done((bf16[1,4,64,128]{3,2,1,0:T(8,128)(2,1)S(1)}, bf16[1,4,64,128]{3,2,1,0:T(8,128)(2,1)S(1)}, u32[]{:S(2)}, u32[]{:S(2)}) %collective-permute-start.5) | collective-permute-done | bytes 65568 | tf_op jit(solution)/shard_map/ppermute | solution.py:489
  46.5 1.5 %collective-permute-start.6 = (bf16[2,2,64,128]{3,2,0,1:T(8,128)(2,1)S(1)}, bf16[2,2,64,128]{3,2,0,1:T(8,128)(2,1)S(1)}, u32[]{:S(2)}, u32[]{:S(2)}) collective-permute-start(bf16[2,2,64,128]{3,2,0,1:T(8,128)(2,1)S(1)} %get-tuple-element.27), channel_id=1, source_target_pairs={{0,8},{4,12},{8,0},{12,4},{16,24},{20,28},{24,16},{28,20},{1,9},{5... | collective-permute-start | bytes 196616 | tf_op jit(solution)/shard_map/ppermute | solution.py:489
  48.0 0.0 collective-permute-done.12
  48.0 1.6 %collective-permute-start.13 = (bf16[64,256]{1,0:T(8,128)(2,1)S(1)}, bf16[64,256]{1,0:T(8,128)(2,1)S(1)}, u32[]{:S(2)}, u32[]{:S(2)}) collective-permute-start(bf16[64,256]{1,0:T(8,128)(2,1)S(1)} %fusion.8), channel_id=1, source_target_pairs={{0,4},{4,0},{8,12},{12,8},{16,20},{20,16},{24,28},{28,24},{1,5},{5... | collective-permute-start | bytes 98312 | tf_op jit(solution)/shard_map/ppermute | solution.py:489
  49.6 1.2 %collective-permute-done.6 = bf16[2,2,64,128]{3,2,0,1:T(8,128)(2,1)S(1)} collective-permute-done((bf16[2,2,64,128]{3,2,0,1:T(8,128)(2,1)S(1)}, bf16[2,2,64,128]{3,2,0,1:T(8,128)(2,1)S(1)}, u32[]{:S(2)}, u32[]{:S(2)}) %collective-permute-start.6) | collective-permute-done | bytes 65568 | tf_op jit(solution)/shard_map/ppermute | solution.py:489
  50.9 1.5 %collective-permute-start.7 = (bf16[4,1,64,128]{3,2,0,1:T(8,128)(2,1)S(1)}, bf16[4,1,64,128]{3,2,0,1:T(8,128)(2,1)S(1)}, u32[]{:S(2)}, u32[]{:S(2)}) collective-permute-start(bf16[4,1,64,128]{3,2,0,1:T(8,128)(2,1)S(1)} %get-tuple-element.26), channel_id=1, source_target_pairs={{0,4},{4,0},{8,12},{12,8},{16,20},{20,16},{24,28},{28,24},{1,5},{5... | collective-permute-start | bytes 196616 | tf_op jit(solution)/shard_map/ppermute | solution.py:489
  52.4 0.0 collective-permute-done.1
  52.4 0.1 add_convert_fusion
  52.5 1.9 %collective-permute-start.2 = (bf16[16,128,128]{2,1,0:T(8,128)(2,1)S(1)}, bf16[16,128,128]{2,1,0:T(8,128)(2,1)S(1)}, u32[]{:S(2)}, u32[]{:S(2)}) collective-permute-start(bf16[16,128,128]{2,1,0:T(8,128)(2,1)S(1)} %add_convert_fusion), channel_id=1, source_target_pairs={{0,2},{1,3},{2,0},{3,1},{4,6},{5,7},{6,4},{7,5},{8,10},{9,11},{10,... | collective-permute-start | bytes 1572872 | tf_op jit(solution)/shard_map/ppermute | solution.py:489
  54.5 0.0 collective-permute-done.13
  54.5 0.1 collective-permute-start.14
  54.6 0.6 collective-permute-done.7
  55.2 0.1 collective-permute-start.8
  55.3 0.5 collective-permute-done.14
  55.8 0.7 %pad_maximum_fusion.1 = f32[128,256]{1,0:T(8,128)} fusion(f32[64,256]{1,0:T(8,128)S(1)} %get-tuple-element.24, f32[64,256]{1,0:T(8,128)S(1)} %get-tuple-element.23), kind=kLoop, calls=%fused_computation.10 | loop fusion | flops 32768 | bytes 262144 | tf_op jit(solution)/shard_map/concatenate | solution.py:507
  56.5 0.1 collective-permute-done.8.there
  56.6 0.0 collective-permute-done.near
  56.6 7.2 %collective-permute-done.2.far = bf16[16,128,128]{2,1,0:T(8,128)(2,1)S(1)} collective-permute-done((bf16[16,128,128]{2,1,0:T(8,128)(2,1)S(1)}, bf16[16,128,128]{2,1,0:T(8,128)(2,1)S(1)}, u32[]{:S(2)}, u32[]{:S(2)}) %collective-permute-start.2) | collective-permute-done | bytes 524320 | tf_op jit(solution)/shard_map/ppermute | solution.py:489
  63.8 1.6 %finish.1 = bf16[2048,128]{1,0:T(8,128)(2,1)} custom-call(s32[1]{0:T(128)} %bitcast.6.mine, s32[1,512]{1,0:T(1,128)S(1)} %reshape.58.index, bf16[16,128,128]{2,1,0:T(8,128)(2,1)S(1)} %get-tuple-element.15.kept, bf16[16,128,128]{2,1,0:T(8,128)(2,1)S(1)} %collective-permute-done.near, bf16[16,128,128]{2,1,0:T(8,128)(2,1)S(1)} %collective-permute-done.2.far, ...), custom_call_target="tpu_custom_call" | custom-call | flops 536870912 | bytes 2621440 | tf_op jit(solution)/shard_map/finish/pallas_call | solution.py:472
  (16 shorter events, 0.2 us)
Async XLA Ops:
  0.6 11.8 %copy-start.1 = (s32[1,8,64]{2,1,0:T(8,128)S(1)}, s32[1,8,64]{2,1,0:T(8,128)}, u32[]{:S(2)}) copy-start(s32[1,8,64]{2,1,0:T(8,128)} %param.11) | copy-start | bytes 6148
  0.6 10.9 %copy-start.2 = (s32[1,8]{1,0:T(1,128)S(1)}, s32[1,8]{1,0:T(1,128)}, u32[]{:S(2)}) copy-start(s32[1,8]{1,0:T(1,128)} %counts_in.1) | copy-start | bytes 100
  3.7 16.5 %all-to-all-start = ((bf16[8,64,128]{2,1,0:T(8,128)(2,1)}), bf16[8,64,128]{2,1,0:T(8,128)(2,1)S(1)}, u32[]{:S(2)}, u32[]{:S(2)}) async-start(bf16[8,64,128]{2,1,0:T(8,128)(2,1)} %bitcast.4), calls=%async_computation | async-start | bytes 262144 | tf_op jit(solution)/shard_map/all_to_all | solution.py:497
  12.7 7.5 %copy-start = (bf16[128,256]{1,0:T(8,128)(2,1)S(1)}, bf16[128,256]{1,0:T(8,128)(2,1)}, u32[]{:S(2)}) copy-start(bf16[128,256]{1,0:T(8,128)(2,1)} %weight.1) | copy-start | bytes 196612
  30.8 25.8 %collective-permute-start = (bf16[16,128,128]{2,1,0:T(8,128)(2,1)S(1)}, bf16[16,128,128]{2,1,0:T(8,128)(2,1)S(1)}, u32[]{:S(2)}, u32[]{:S(2)}) collective-permute-start(bf16[16,128,128]{2,1,0:T(8,128)(2,1)S(1)} %get-tuple-element.16), channel_id=1, source_target_pairs={{0,1},{1,0},{2,3},{3,2},{4,5},{5,4},{6,7},{7,6},{8,9},{9,8},{10,11... | collective-permute-start | bytes 1572872 | tf_op jit(solution)/shard_map/ppermute | solution.py:489
  30.9 21.5 %collective-permute-start.1 = (bf16[16,128,128]{2,1,0:T(8,128)(2,1)S(1)}, bf16[16,128,128]{2,1,0:T(8,128)(2,1)S(1)}, u32[]{:S(2)}, u32[]{:S(2)}) collective-permute-start(bf16[16,128,128]{2,1,0:T(8,128)(2,1)S(1)} %get-tuple-element.18), channel_id=1, source_target_pairs={{0,1},{1,0},{2,3},{3,2},{4,5},{5,4},{6,7},{7,6},{8,9},{9,8},{10,11... | collective-permute-start | bytes 1572872 | tf_op jit(solution)/shard_map/ppermute | solution.py:489
  31.4 2.2 %collective-permute-start.9 = (f32[64,256]{1,0:T(8,128)S(1)}, f32[64,256]{1,0:T(8,128)S(1)}, u32[]{:S(2)}, u32[]{:S(2)}) collective-permute-start(f32[64,256]{1,0:T(8,128)S(1)} %dynamic-slice_bitcast_fusion), channel_id=1, source_target_pairs={{0,1},{1,0},{2,3},{3,2},{4,5},{5,4},{6,7},{7,6},{8,9},{9,8},{10,11... | collective-permute-start | bytes 196616 | tf_op jit(solution)/shard_map/ppermute | solution.py:489
  31.5 3.8 %collective-permute-start.3 = (bf16[256,128]{1,0:T(8,128)(2,1)S(1)}, bf16[256,128]{1,0:T(8,128)(2,1)S(1)}, u32[]{:S(2)}, u32[]{:S(2)}) collective-permute-start(bf16[256,128]{1,0:T(8,128)(2,1)S(1)} %dynamic-slice_bitcast_fusion.1), channel_id=1, source_target_pairs={{0,1},{1,0},{2,3},{3,2},{4,5},{5,4},{6,7},{7,6},{8,9},{9,8},{10,11... | collective-permute-start | bytes 196616 | tf_op jit(solution)/shard_map/ppermute | solution.py:489
  33.7 4.5 %collective-permute-start.10 = (f32[64,256]{1,0:T(8,128)S(1)}, f32[64,256]{1,0:T(8,128)S(1)}, u32[]{:S(2)}, u32[]{:S(2)}) collective-permute-start(f32[64,256]{1,0:T(8,128)S(1)} %bitcast_add_fusion), channel_id=1, source_target_pairs={{0,2},{1,3},{2,0},{3,1},{4,6},{5,7},{6,4},{7,5},{8,10},{9,11},{10,... | collective-permute-start | bytes 196616 | tf_op jit(solution)/shard_map/ppermute | solution.py:489
  35.3 5.9 %collective-permute-start.4 = (bf16[256,128]{1,0:T(8,128)(2,1)S(1)}, bf16[256,128]{1,0:T(8,128)(2,1)S(1)}, u32[]{:S(2)}, u32[]{:S(2)}) collective-permute-start(bf16[256,128]{1,0:T(8,128)(2,1)S(1)} %fusion), channel_id=1, source_target_pairs={{0,2},{1,3},{2,0},{3,1},{4,6},{5,7},{6,4},{7,5},{8,10},{9,11},{10,... | collective-permute-start | bytes 196616 | tf_op jit(solution)/shard_map/ppermute | solution.py:489
  38.2 5.0 %collective-permute-start.11 = (bf16[64,256]{1,0:T(8,128)(2,1)S(1)}, bf16[64,256]{1,0:T(8,128)(2,1)S(1)}, u32[]{:S(2)}, u32[]{:S(2)}) collective-permute-start(bf16[64,256]{1,0:T(8,128)(2,1)S(1)} %get-tuple-element.21), channel_id=1, source_target_pairs={{0,16},{4,20},{8,24},{12,28},{16,0},{20,4},{24,8},{28,12},{1,17},{... | collective-permute-start | bytes 98312 | tf_op jit(solution)/shard_map/ppermute | solution.py:489
  41.3 5.2 %collective-permute-start.5 = (bf16[1,4,64,128]{3,2,1,0:T(8,128)(2,1)S(1)}, bf16[1,4,64,128]{3,2,1,0:T(8,128)(2,1)S(1)}, u32[]{:S(2)}, u32[]{:S(2)}) collective-permute-start(bf16[1,4,64,128]{3,2,1,0:T(8,128)(2,1)S(1)} %bitcast.38), channel_id=1, source_target_pairs={{0,16},{4,20},{8,24},{12,28},{16,0},{20,4},{24,8},{28,12},{1,17},{... | collective-permute-start | bytes 196616 | tf_op jit(solution)/shard_map/ppermute | solution.py:489
  43.1 4.9 %collective-permute-start.12 = (bf16[64,256]{1,0:T(8,128)(2,1)S(1)}, bf16[64,256]{1,0:T(8,128)(2,1)S(1)}, u32[]{:S(2)}, u32[]{:S(2)}) collective-permute-start(bf16[64,256]{1,0:T(8,128)(2,1)S(1)} %fusion.7), channel_id=1, source_target_pairs={{0,8},{4,12},{8,0},{12,4},{16,24},{20,28},{24,16},{28,20},{1,9},{5... | collective-permute-start | bytes 98312 | tf_op jit(solution)/shard_map/ppermute | solution.py:489
  46.5 4.3 %collective-permute-start.6 = (bf16[2,2,64,128]{3,2,0,1:T(8,128)(2,1)S(1)}, bf16[2,2,64,128]{3,2,0,1:T(8,128)(2,1)S(1)}, u32[]{:S(2)}, u32[]{:S(2)}) collective-permute-start(bf16[2,2,64,128]{3,2,0,1:T(8,128)(2,1)S(1)} %get-tuple-element.27), channel_id=1, source_target_pairs={{0,8},{4,12},{8,0},{12,4},{16,24},{20,28},{24,16},{28,20},{1,9},{5... | collective-permute-start | bytes 196616 | tf_op jit(solution)/shard_map/ppermute | solution.py:489
  48.0 6.4 %collective-permute-start.13 = (bf16[64,256]{1,0:T(8,128)(2,1)S(1)}, bf16[64,256]{1,0:T(8,128)(2,1)S(1)}, u32[]{:S(2)}, u32[]{:S(2)}) collective-permute-start(bf16[64,256]{1,0:T(8,128)(2,1)S(1)} %fusion.8), channel_id=1, source_target_pairs={{0,4},{4,0},{8,12},{12,8},{16,20},{20,16},{24,28},{28,24},{1,5},{5... | collective-permute-start | bytes 98312 | tf_op jit(solution)/shard_map/ppermute | solution.py:489
  50.9 4.3 %collective-permute-start.7 = (bf16[4,1,64,128]{3,2,0,1:T(8,128)(2,1)S(1)}, bf16[4,1,64,128]{3,2,0,1:T(8,128)(2,1)S(1)}, u32[]{:S(2)}, u32[]{:S(2)}) collective-permute-start(bf16[4,1,64,128]{3,2,0,1:T(8,128)(2,1)S(1)} %get-tuple-element.26), channel_id=1, source_target_pairs={{0,4},{4,0},{8,12},{12,8},{16,20},{20,16},{24,28},{28,24},{1,5},{5... | collective-permute-start | bytes 196616 | tf_op jit(solution)/shard_map/ppermute | solution.py:489
  52.5 11.3 %collective-permute-start.2 = (bf16[16,128,128]{2,1,0:T(8,128)(2,1)S(1)}, bf16[16,128,128]{2,1,0:T(8,128)(2,1)S(1)}, u32[]{:S(2)}, u32[]{:S(2)}) collective-permute-start(bf16[16,128,128]{2,1,0:T(8,128)(2,1)S(1)} %add_convert_fusion), channel_id=1, source_target_pairs={{0,2},{1,3},{2,0},{3,1},{4,6},{5,7},{6,4},{7,5},{8,10},{9,11},{10,... | collective-permute-start | bytes 1572872 | tf_op jit(solution)/shard_map/ppermute | solution.py:489
  54.5 1.3 %collective-permute-start.14 = (f32[64,256]{1,0:T(8,128)S(1)}, f32[64,256]{1,0:T(8,128)S(1)}, u32[]{:S(2)}, u32[]{:S(2)}) collective-permute-start(f32[64,256]{1,0:T(8,128)S(1)} %convert_add_fusion.1), channel_id=1, source_target_pairs={{0,1},{1,0},{2,3},{3,2},{4,5},{5,4},{6,7},{7,6},{8,9},{9,8},{10,11... | collective-permute-start | bytes 196616 | tf_op jit(solution)/shard_map/ppermute | solution.py:489
  55.2 1.4 %collective-permute-start.8 = (bf16[512,128]{1,0:T(8,128)(2,1)S(1)}, bf16[512,128]{1,0:T(8,128)(2,1)S(1)}, u32[]{:S(2)}, u32[]{:S(2)}) collective-permute-start(bf16[512,128]{1,0:T(8,128)(2,1)S(1)} %bitcast.31), channel_id=1, source_target_pairs={{0,1},{1,0},{2,3},{3,2},{4,5},{5,4},{6,7},{7,6},{8,9},{9,8},{10,11... | collective-permute-start | bytes 393224 | tf_op jit(solution)/shard_map/ppermute | solution.py:489
